TPU v7x, 32 devices: a whole 2x2x4 slice. The times are simulated.
32 devices in a mesh: seq: 4 (over z), batch: 4 (over x, core), tensor: 2 (over y).
Axes of the slice: x: 2, y: 2, z: 4, core: 2. Of those that a mesh axis runs over, the one named last changes fastest.
Arguments:
- inputs: bfloat16 [4, 1024, 768], P('batch', 'seq'), may hold values from -16 to 16
- history: bfloat16 [8, 4, 1024, 768], P(None, 'batch', 'seq'), may hold values from -6 to 6
- window_lengths: int32 [4, 3], P('batch'), may hold values from 1 to 768, 1024 in all within a row
- block_order: int32 [4], replicated, may hold values from 0 to 3, each once
- first_gain: float32 [768], replicated, may hold values from 0.5 to 1.5
- first_shift: float32 [768], replicated, may hold values from -1.5 to 1.5
- query_weight: bfloat16 [768, 768], P(None, 'tensor'), may hold values from -0.21875 to 0.21875
- key_weight: bfloat16 [768, 768], P(None, 'tensor'), may hold values from -0.21875 to 0.21875
- value_weight: bfloat16 [768, 768], P(None, 'tensor'), may hold values from -0.21875 to 0.21875
- out_weight: bfloat16 [768, 768], P('tensor'), may hold values from -1.75 to 1.75
- second_gain: float32 [768], replicated, may hold values from 0.5 to 1.5
- second_shift: float32 [768], replicated, may hold values from -1.5 to 1.5
- up_weight: bfloat16 [768, 3072], P(None, 'tensor'), may hold values from -0.21875 to 0.21875
- up_bias: float32 [3072], P('tensor'), may hold values from -2.5 to 2.5
- down_weight: bfloat16 [3072, 768], P('tensor'), may hold values from -0.109375 to 0.109375
- down_bias: float32 [768], replicated, may hold values from -1.5 to 1.5
- mix_weights: float32 [9], replicated, may hold values from -2.5 to 2.5
- cotangent_next: bfloat16 [4, 1024, 768], P('batch', 'seq'), may hold values from -6 to 6
- cotangent_block: bfloat16 [4, 1024, 768], P('batch', 'seq'), may hold values from -6 to 6
Outputs:
- next_input: bfloat16 [4, 1024, 768], P('batch', 'seq')
- block_output: bfloat16 [4, 1024, 768], P('batch', 'seq')
- grad_input: bfloat16 [4, 1024, 768], P('batch', 'seq')
- grad_history: bfloat16 [8, 4, 1024, 768], P(None, 'batch', 'seq')
- grad_first_gain: float32 [768], replicated
- grad_first_shift: float32 [768], replicated
- grad_query_weight: float32 [768, 768], P(('seq', 'batch'), 'tensor')
- grad_key_weight: float32 [768, 768], P(('seq', 'batch'), 'tensor')
- grad_value_weight: float32 [768, 768], P(('seq', 'batch'), 'tensor')
- grad_out_weight: float32 [768, 768], P('tensor', ('seq', 'batch'))
- grad_second_gain: float32 [768], replicated
- grad_second_shift: float32 [768], replicated
- grad_up_weight: float32 [768, 3072], P(('seq', 'batch'), 'tensor')
- grad_up_bias: float32 [3072], P('tensor')
- grad_down_weight: float32 [3072, 768], P('tensor', ('seq', 'batch'))
- grad_down_bias: float32 [768], replicated
- grad_mix_weights: float32 [9], replicated
- rms_values: float32 [3], replicated
Inputs may be any that keep to these rules, and one draw needn't show every extreme that they name: `window_lengths`: each row sums to 1024; the longest window of each row has exactly 768 tokens. A permutation; index i of seq holds positions block_order[i] * 256 to block_order[i] * 256 + 255 of each sequence.
All inputs are finite; a program needn't handle non-finite values.
Results may differ from a plain program's by a relative error of at most 0.025.
Values may be sent and summed in bfloat16 or wider, within the bound.
A program may use at most 192 MiB of HBM per device.

v0:
```python
import jax
import jax.numpy as jnp
from jax import lax
from jax.sharding import PartitionSpec as P

HEAD_DIM = 64


epsilon = 1e-05


def layer_parts(values, gain, shift):
    centre = jnp.mean(values, axis=-1, keepdims=True)
    centred = values - centre
    spread = jnp.mean(centred * centred, axis=-1, keepdims=True)
    inverse = lax.rsqrt(spread + epsilon)
    unit = centred * inverse
    return (unit * gain + shift, unit, inverse)


def norm_backward(grad_out, unit, inverse, gain):
    scaled = grad_out * gain
    return inverse * (
        scaled
        - jnp.mean(scaled, axis=-1, keepdims=True)
        - unit * jnp.mean(scaled * unit, axis=-1, keepdims=True)
    )


def gelu_tanh(values):
    return (
        0.5
        * values
        * (1.0 + jnp.tanh(0.7978845608028654 * (values + 0.044715 * values * values * values)))
    )


def rotate(values, cosine, sine):
    half = values.shape[-1] // 2
    first = values[..., :half]
    second = values[..., half:]
    return jnp.concatenate(
        [first * cosine - second * sine, second * cosine + first * sine], axis=-1
    )


def keep_state(state):
    return state


def per_device(
    inputs,
    history,
    window_lengths,
    block_order,
    first_gain,
    first_shift,
    query_weight,
    key_weight,
    value_weight,
    out_weight,
    second_gain,
    second_shift,
    up_weight,
    up_bias,
    down_weight,
    down_bias,
    mix_weights,
    cotangent_next,
    cotangent_block,
):
    rows = inputs.shape[1]
    width = inputs.shape[2]
    local_width = query_weight.shape[1]
    heads = local_width // HEAD_DIM
    half = HEAD_DIM // 2
    depth = history.shape[0]
    total = rows * lax.axis_size("seq")
    size = min(1024, total)
    count = total // size
    split = (rows, heads, HEAD_DIM)
    offsets = jnp.arange(rows, dtype=jnp.int32)
    own_pos = block_order[lax.axis_index("seq")] * rows + offsets
    every_row = jnp.arange(total, dtype=jnp.int32)
    every_pos = block_order[every_row // rows] * rows + every_row % rows
    ends = jnp.cumsum(window_lengths[0])
    own_docs = jnp.sum((own_pos[:, None] >= ends[None, :]).astype(jnp.int32), axis=1)
    every_docs = jnp.sum((every_pos[:, None] >= ends[None, :]).astype(jnp.int32), axis=1)
    rates = jnp.exp(-jnp.log(10000.0) * jnp.arange(half, dtype=jnp.float32) / half)
    angles = own_pos.astype(jnp.float32)[:, None] * rates[None, :]
    cosine = jnp.cos(angles)[:, None, :]
    sine = jnp.sin(angles)[:, None, :]
    residual = inputs[0].astype(jnp.float32)
    normed_first, unit_first, scale_first = layer_parts(residual, first_gain, first_shift)
    normed_first = normed_first.astype(jnp.bfloat16)
    query_lin = jnp.dot(normed_first, query_weight, preferred_element_type=jnp.float32)
    key_lin = jnp.dot(normed_first, key_weight, preferred_element_type=jnp.float32)
    value_lin = jnp.dot(normed_first, value_weight, preferred_element_type=jnp.float32)
    queries = (rotate(query_lin.reshape(split), cosine, sine) * 0.125).astype(jnp.bfloat16)
    keys = (
        rotate(key_lin.reshape(split), cosine, sine).reshape(rows, local_width).astype(jnp.bfloat16)
    )
    values = value_lin.astype(jnp.bfloat16)
    all_keys, all_values = (
        lax.all_gather(keys, "seq", axis=0, tiled=True),
        lax.all_gather(values, "seq", axis=0, tiled=True),
    )

    def block_mask(index):
        key_pos = lax.dynamic_slice_in_dim(every_pos, index * size, size)
        key_docs = lax.dynamic_slice_in_dim(every_docs, index * size, size)
        return (key_pos[None, :] <= own_pos[:, None]) & (key_docs[None, :] == own_docs[:, None])

    def block_rows(array, index):
        return lax.dynamic_slice_in_dim(array, index * size, size).reshape(size, heads, HEAD_DIM)

    def block_scores(index, key_rows):
        return jnp.einsum(
            "qhd,khd->hqk", queries, block_rows(key_rows, index), preferred_element_type=jnp.float32
        )

    def stats_step(index, carry):
        allowed = block_mask(index)

        def update(state):
            peak, denom = state
            masked = jnp.where(allowed[None], block_scores(index, all_keys), -1e30)
            fresh = jnp.maximum(peak, jnp.max(masked, axis=-1))
            weights = jnp.where(allowed[None], jnp.exp(masked - fresh[..., None]), 0.0)
            return (fresh, denom * jnp.exp(peak - fresh) + jnp.sum(weights, axis=-1))

        return lax.cond(jnp.any(allowed), update, keep_state, carry)

    start_stats = (
        jnp.full((heads, rows), -1e30, jnp.float32),
        jnp.zeros((heads, rows), jnp.float32),
    )
    peak, denom = lax.fori_loop(0, count, stats_step, start_stats)

    def block_probs(index, allowed, key_rows):
        scores = block_scores(index, key_rows)
        return jnp.where(allowed[None], jnp.exp(scores - peak[..., None]), 0.0) / denom[..., None]

    def output_step(index, carry):
        allowed = block_mask(index)

        def output_accumulate(state):
            probs_low = block_probs(index, allowed, all_keys).astype(jnp.bfloat16)
            return state + jnp.einsum(
                "hqk,khd->qhd",
                probs_low,
                block_rows(all_values, index),
                preferred_element_type=jnp.float32,
            )

        return lax.cond(jnp.any(allowed), output_accumulate, keep_state, carry)

    running = lax.fori_loop(0, count, output_step, jnp.zeros(split, jnp.float32))
    mixed = running.reshape(rows, local_width).astype(jnp.bfloat16)
    attn_out = lax.psum(
        jnp.dot(mixed, out_weight, preferred_element_type=jnp.float32).astype(jnp.bfloat16),
        "tensor",
    ).astype(jnp.float32)
    hidden = residual + attn_out
    normed_second, unit_second, scale_second = layer_parts(hidden, second_gain, second_shift)
    normed_second = normed_second.astype(jnp.bfloat16)
    upward = jnp.dot(normed_second, up_weight, preferred_element_type=jnp.float32) + up_bias
    active_full, gelu_pull = jax.vjp(gelu_tanh, upward)
    active = active_full.astype(jnp.bfloat16)
    mlp_out = (
        lax.psum(
            jnp.dot(active, down_weight, preferred_element_type=jnp.float32).astype(jnp.bfloat16),
            "tensor",
        ).astype(jnp.float32)
        + down_bias
    )
    block_value = hidden + mlp_out
    history_low = history[:, 0]
    next_value = (
        jnp.sum(mix_weights[:depth, None, None] * history_low.astype(jnp.float32), axis=0)
        + mix_weights[depth] * block_value
    )
    cot_low = cotangent_next[0]
    cot_next = cot_low.astype(jnp.float32)
    cot_block = cotangent_block[0].astype(jnp.float32)
    grad_history = (mix_weights[:depth, None, None] * cot_next[None]).astype(jnp.bfloat16)
    mix_terms = jnp.concatenate(
        [
            jnp.einsum("jsd,sd->j", history_low, cot_low, preferred_element_type=jnp.float32),
            jnp.sum(block_value * cot_next)[None],
        ]
    )
    grad_block = cot_block + mix_weights[depth] * cot_next
    grad_mlp = grad_block.astype(jnp.bfloat16)
    grad_down = jnp.einsum("sf,sd->fd", active, grad_mlp, preferred_element_type=jnp.float32)
    grad_active = jnp.einsum("sd,fd->sf", grad_mlp, down_weight, preferred_element_type=jnp.float32)
    grad_up = gelu_pull(grad_active)[0].astype(jnp.bfloat16)
    grad_upw = jnp.einsum("sd,sf->df", normed_second, grad_up, preferred_element_type=jnp.float32)
    grad_normed_second = lax.psum(
        jnp.einsum("sf,df->sd", grad_up, up_weight, preferred_element_type=jnp.float32).astype(
            jnp.bfloat16
        ),
        "tensor",
    ).astype(jnp.float32)
    grad_hidden = grad_block + norm_backward(
        grad_normed_second, unit_second, scale_second, second_gain
    )
    grad_attn = grad_hidden.astype(jnp.bfloat16)
    grad_outw = jnp.einsum("sk,sd->kd", mixed, grad_attn, preferred_element_type=jnp.float32)
    grad_mixed = (
        jnp.einsum("sd,kd->sk", grad_attn, out_weight, preferred_element_type=jnp.float32)
        .astype(jnp.bfloat16)
        .reshape(split)
    )
    back_keys, back_values = (
        lax.all_gather(keys, "seq", axis=0, tiled=True),
        lax.all_gather(values, "seq", axis=0, tiled=True),
    )

    def delta_step(index, carry):
        allowed = block_mask(index)

        def delta_accumulate(state):
            probs = block_probs(index, allowed, back_keys)
            grad_probs = jnp.einsum(
                "qhd,khd->hqk",
                grad_mixed,
                block_rows(back_values, index),
                preferred_element_type=jnp.float32,
            )
            return state + jnp.sum(probs * grad_probs, axis=-1)

        return lax.cond(jnp.any(allowed), delta_accumulate, keep_state, carry)

    delta = lax.fori_loop(0, count, delta_step, jnp.zeros((heads, rows), jnp.float32))

    def grad_step(index, carry):
        allowed = block_mask(index)

        def grad_accumulate(state):
            grad_queries, key_buffer, value_buffer = state
            key_rows = block_rows(back_keys, index)
            value_rows = block_rows(back_values, index)
            probs = block_probs(index, allowed, back_keys)
            grad_probs = jnp.einsum(
                "qhd,khd->hqk", grad_mixed, value_rows, preferred_element_type=jnp.float32
            )
            grad_scores = (probs * (grad_probs - delta[..., None])).astype(jnp.bfloat16)
            grad_queries = grad_queries + jnp.einsum(
                "hqk,khd->qhd", grad_scores, key_rows, preferred_element_type=jnp.float32
            )
            key_part = jnp.einsum(
                "hqk,qhd->khd", grad_scores, queries, preferred_element_type=jnp.float32
            ).reshape(size, local_width)
            value_part = jnp.einsum(
                "hqk,qhd->khd",
                probs.astype(jnp.bfloat16),
                grad_mixed,
                preferred_element_type=jnp.float32,
            ).reshape(size, local_width)
            key_buffer = lax.dynamic_update_slice_in_dim(key_buffer, key_part, index * size, 0)
            value_buffer = lax.dynamic_update_slice_in_dim(
                value_buffer, value_part, index * size, 0
            )
            return (grad_queries, key_buffer, value_buffer)

        return lax.cond(jnp.any(allowed), grad_accumulate, keep_state, carry)

    start_grads = (
        jnp.zeros(split, jnp.float32),
        jnp.zeros((total, local_width), jnp.float32),
        jnp.zeros((total, local_width), jnp.float32),
    )
    grad_queries, key_buffer, value_buffer = lax.fori_loop(0, count, grad_step, start_grads)
    grad_keys, grad_values = (
        lax.psum_scatter(
            key_buffer.astype(jnp.bfloat16), "seq", scatter_dimension=0, tiled=True
        ).astype(jnp.float32),
        lax.psum_scatter(
            value_buffer.astype(jnp.bfloat16), "seq", scatter_dimension=0, tiled=True
        ).astype(jnp.float32),
    )
    grad_query_lin = (
        rotate(grad_queries * 0.125, cosine, -sine).reshape(rows, local_width).astype(jnp.bfloat16)
    )
    grad_key_lin = (
        rotate(grad_keys.reshape(split), cosine, -sine)
        .reshape(rows, local_width)
        .astype(jnp.bfloat16)
    )
    grad_value_lin = grad_values.astype(jnp.bfloat16)
    grad_queryw = jnp.einsum(
        "sd,se->de", normed_first, grad_query_lin, preferred_element_type=jnp.float32
    )
    grad_keyw = jnp.einsum(
        "sd,se->de", normed_first, grad_key_lin, preferred_element_type=jnp.float32
    )
    grad_valuew = jnp.einsum(
        "sd,se->de", normed_first, grad_value_lin, preferred_element_type=jnp.float32
    )
    local_normed = jnp.einsum(
        "se,de->sd", grad_query_lin, query_weight, preferred_element_type=jnp.float32
    )
    local_normed = local_normed + jnp.einsum(
        "se,de->sd", grad_key_lin, key_weight, preferred_element_type=jnp.float32
    )
    local_normed = local_normed + jnp.einsum(
        "se,de->sd", grad_value_lin, value_weight, preferred_element_type=jnp.float32
    )
    grad_normed_first = lax.psum(local_normed.astype(jnp.bfloat16), "tensor").astype(jnp.float32)
    grad_input = grad_hidden + norm_backward(grad_normed_first, unit_first, scale_first, first_gain)
    shared_grads = (
        lax.psum_scatter(grad_queryw, ("seq", "batch"), scatter_dimension=0, tiled=True),
        lax.psum_scatter(grad_keyw, ("seq", "batch"), scatter_dimension=0, tiled=True),
        lax.psum_scatter(grad_valuew, ("seq", "batch"), scatter_dimension=0, tiled=True),
        lax.psum_scatter(grad_outw, ("seq", "batch"), scatter_dimension=1, tiled=True),
        lax.psum_scatter(grad_upw, ("seq", "batch"), scatter_dimension=0, tiled=True),
        lax.psum_scatter(grad_down, ("seq", "batch"), scatter_dimension=1, tiled=True),
    )
    square_terms = jnp.stack(
        [
            jnp.sum(block_value * block_value),
            jnp.sum(attn_out * attn_out),
            jnp.sum(mlp_out * mlp_out),
        ]
    )
    small_terms = lax.psum(
        (
            jnp.sum(grad_normed_first * unit_first, axis=0),
            jnp.sum(grad_normed_first, axis=0),
            jnp.sum(grad_normed_second * unit_second, axis=0),
            jnp.sum(grad_normed_second, axis=0),
            jnp.sum(grad_up.astype(jnp.float32), axis=0),
            jnp.sum(grad_mlp.astype(jnp.float32), axis=0),
            mix_terms,
            square_terms,
        ),
        ("seq", "batch"),
    )
    entries = float(lax.axis_size("batch") * total * width)
    rms_values = jnp.sqrt(small_terms[7] / entries)
    return (
        next_value.astype(jnp.bfloat16)[None],
        block_value.astype(jnp.bfloat16)[None],
        grad_input.astype(jnp.bfloat16)[None],
        grad_history[:, None],
        small_terms[0],
        small_terms[1],
        shared_grads[0],
        shared_grads[1],
        shared_grads[2],
        shared_grads[3],
        small_terms[2],
        small_terms[3],
        shared_grads[4],
        small_terms[4],
        shared_grads[5],
        small_terms[5],
        small_terms[6],
        rms_values,
    )


def solution(mesh):
    in_specs = (
        P("batch", "seq", None),
        P(None, "batch", "seq", None),
        P("batch", None),
        P(),
        P(),
        P(),
        P(None, "tensor"),
        P(None, "tensor"),
        P(None, "tensor"),
        P("tensor", None),
        P(),
        P(),
        P(None, "tensor"),
        P("tensor"),
        P("tensor", None),
        P(),
        P(),
        P("batch", "seq", None),
        P("batch", "seq", None),
    )
    out_specs = (
        P("batch", "seq", None),
        P("batch", "seq", None),
        P("batch", "seq", None),
        P(None, "batch", "seq", None),
        P(),
        P(),
        P(("seq", "batch"), "tensor"),
        P(("seq", "batch"), "tensor"),
        P(("seq", "batch"), "tensor"),
        P("tensor", ("seq", "batch")),
        P(),
        P(),
        P(("seq", "batch"), "tensor"),
        P("tensor"),
        P("tensor", ("seq", "batch")),
        P(),
        P(),
        P(),
    )
    return jax.shard_map(
        per_device, mesh=mesh, in_specs=in_specs, out_specs=out_specs, check_vma=False
    )
```

profile of v0, /device:TPU:0, one launch (start us, length us, event | category | flops | bytes accessed | tf_op | source)
XLA Modules:
  0.0 684.2 jit_solution(1408262053932993367)
XLA Ops:
  22.0 21.7 %all_gather.8 = bf16[1024,384]{0,1:T(8,128)(2,1)} all-gather(bf16[256,384]{0,1:T(8,128)(2,1)S(1)} %bitcast.211), channel_id=1, replica_groups=mesh['seq'=4,'batch'=4,'tensor'=2] {'seq'}, dimensions={0}, use_global_device_ids=true | all-gather | bytes 983040 | tf_op jit(solution)/shard_map/all_gather | solution.py:105
  49.5 17.3 %all_gather.9 = bf16[1024,384]{1,0:T(8,128)(2,1)S(1)} all-gather(bf16[256,384]{1,0:T(8,128)(2,1)S(1)} %convolution_convert_fusion.4), channel_id=1, replica_groups=mesh['seq'=4,'batch'=4,'tensor'=2] {'seq'}, dimensions={0}, use_global_device_ids=true | all-gather | bytes 983040 | tf_op jit(solution)/shard_map/all_gather | solution.py:106
  68.1 6.7 conditional.4
  75.6 6.0 conditional.5
  76.7 4.8 fusion.4
  87.0 3.2 convert_reduce_fusion.4
  90.3 21.2 %all-reduce.6.cloned.1.call-done = bf16[256,768]{1,0:T(8,128)(2,1)} async-done(((bf16[256,768]{1,0:T(8,128)(2,1)}), bf16[256,768]{1,0:T(8,128)(2,1)}) %all-reduce.6.cloned.1.call-update) | async-done | bytes 393232 | tf_op jit(solution)/shard_map/psum | solution.py:160
  126.8 31.8 %all-reduce.10.cloned.1.call-done = (bf16[256,768]{1,0:T(8,128)(2,1)}, bf16[256,768]{1,0:T(8,128)(2,1)}) async-done(((bf16[256,768]{1,0:T(8,128)(2,1)}, bf16[256,768]{1,0:T(8,128)(2,1)}), (bf16[256,768]{1,0:T(8,128)(2,1)}, bf16[256,768]{1,0:T(8,128)(2,1)})) %all-reduce.10.cloned.1.call-update) | async-done | bytes 786448 | tf_op jit(solution)/shard_map/psum | solution.py:171
  158.7 4.3 multiply_reduce_fusion.4
  167.0 11.1 %conditional.6 = (f32[6,256]{1,0:T(8,128)S(1)}) conditional(s32[]{:T(128)} %convert_element_type.198, f32[6,256]{1,0:T(8,128)S(1)} %broadcast.362, (pred[256,1024]{1,0:T(8,128)(4,1)}, bf16[1024,384]{0,1:T(8,128)(2,1)S(1)}, bf16[256,6,64]{0,2,1:T(8,128)(2,1)}, f32[6,256]{1,0:T(8,128)}, f32[6,256]{1,0:T(8,128)}, ...), branch_computations={%region_20.21_spmd, %region_21.23_spmd} | conditional | flops 410517504 | bytes 16420872 | solution.py:233
  167.0 4.6 fusion.84
  172.8 5.3 multiply_reduce_fusion
  178.1 17.4 %conditional.7 = (f32[256,6,64]{0,2,1:T(8,128)}, bf16[1024,384]{0,1:T(8,128)(2,1)}, bf16[1024,384]{0,1:T(8,128)(2,1)S(1)}) conditional(s32[]{:T(128)} %convert_element_type.198, f32[256,6,64]{0,2,1:T(8,128)} %broadcast.358, (pred[256,1024]{1,0:T(8,128)(4,1)}, bf16[1024,384]{0,1:T(8,128)(2,1)S(1)}, bf16[256,6,64]{0,2,1:T(8,128)(2,1)}, ...), branch_computations={%region_23.24_spmd, %region_24.25_spmd} | conditional | flops 1017741312 | bytes 61622352 | solution.py:267
  178.4 5.5 select_divide_fusion
  185.1 4.2 multiply_convert_fusion
  197.5 21.5 %reduce-scatter.9.cloned.1.call-done = bf16[256,384]{0,1:T(8,128)(2,1)} async-done(((bf16[1024,384]{0,1:T(8,128)(2,1)}), bf16[256,384]{0,1:T(8,128)(2,1)}) %reduce-scatter.9.cloned.1.call-update) | async-done | bytes 196624 | tf_op jit(solution)/shard_map/reduce_scatter | solution.py:276
  222.4 21.4 %reduce-scatter.11.cloned.1.call-done = bf16[256,384]{0,1:T(8,128)(2,1)} async-done(((bf16[1024,384]{0,1:T(8,128)(2,1)}), bf16[256,384]{0,1:T(8,128)(2,1)}) %reduce-scatter.11.cloned.1.call-update) | async-done | bytes 196624 | tf_op jit(solution)/shard_map/reduce_scatter | solution.py:279
  257.4 3.1 fusion.75
  273.5 62.1 %all-reduce = (f32[768]{0:T(1024)}, f32[768]{0:T(1024)}, f32[768]{0:T(1024)}, f32[768]{0:T(1024)}, f32[1536]{0:T(1024)}, /*index=5*/f32[768]{0:T(1024)}, f32[9]{0:T(128)}, f32[3]{0:T(128)}) all-reduce(f32[768]{0:T(1024)} %get-tuple-element.439, ...), channel_id=1, replica_groups=mesh['seq'=4,'batch'=4,'tensor'=2] {'seq','batch'}, use_global_device_ids=true, to_apply=%region_31.32 | all-reduce | flops 5388 | bytes 43104 | tf_op jit(solution)/shard_map/psum | solution.py:327
  340.1 55.5 %reduce-scatter.15.cloned.1.call-done = f32[48,384]{1,0:T(8,128)} async-done(((f32[768,384]{1,0:T(8,128)}), f32[48,384]{1,0:T(8,128)}) %reduce-scatter.15.cloned.1.call-update) | async-done | bytes 73744 | tf_op jit(solution)/shard_map/reduce_scatter | solution.py:314
  395.6 61.9 %reduce-scatter.13.cloned.1.call-done = f32[48,384]{1,0:T(8,128)} async-done(((f32[768,384]{1,0:T(8,128)}), f32[48,384]{1,0:T(8,128)}) %reduce-scatter.13.cloned.1.call-update) | async-done | bytes 73744 | tf_op jit(solution)/shard_map/reduce_scatter | solution.py:313
  457.5 61.7 %reduce-scatter.17.cloned.1.call-done = f32[48,384]{1,0:T(8,128)} async-done(((f32[768,384]{1,0:T(8,128)}), f32[48,384]{1,0:T(8,128)}) %reduce-scatter.17.cloned.1.call-update) | async-done | bytes 73744 | tf_op jit(solution)/shard_map/reduce_scatter | solution.py:315
  519.2 79.4 %reduce-scatter.21.cloned.1.call-done = f32[48,1536]{1,0:T(8,128)} async-done(((f32[768,1536]{1,0:T(8,128)}), f32[48,1536]{1,0:T(8,128)}) %reduce-scatter.21.cloned.1.call-update) | async-done | bytes 294928 | tf_op jit(solution)/shard_map/reduce_scatter | solution.py:317
  598.6 79.1 %reduce-scatter.23.cloned.1.call-done = f32[1536,48]{0,1:T(8,128)} async-done(((f32[1536,768]{0,1:T(8,128)}), f32[1536,48]{0,1:T(8,128)}) %reduce-scatter.23.cloned.1.call-update) | async-done | bytes 294928 | tf_op jit(solution)/shard_map/reduce_scatter | solution.py:318
  (227 shorter events, 98.3 us)
Async XLA Ops:
  7.2 110.0 %copy-start = (bf16[1536,768]{1,0:T(8,128)(2,1)S(1)}, bf16[1536,768]{1,0:T(8,128)(2,1)}, u32[]{:S(2)}) copy-start(bf16[1536,768]{1,0:T(8,128)(2,1)} %param.41) | copy-start | bytes 7077892
  7.3 104.2 %all-reduce.6.cloned.1.call-start = ((), (), s32[]{:S(2)}) async-start(), calls=%async_computation.8 | async-start | bytes 786432 | tf_op jit(solution)/shard_map/psum | solution.py:160
  8.7 40.3 %copy-start.41 = (f32[256]{0:T(256)}, f32[256]{0:T(256)S(1)}, u32[]{:S(2)}) copy-start(f32[256]{0:T(256)S(1)} %broadcast_multiply_fusion.6) | copy-start | bytes 3076
  9.9 39.0 %copy-start.45 = (f32[256]{0:T(256)}, f32[256]{0:T(256)S(1)}, u32[]{:S(2)}) copy-start(f32[256]{0:T(256)S(1)} %add_rsqrt_fusion.1) | copy-start | bytes 3076
  15.4 33.5 %copy-start.34 = (bf16[768,384]{1,0:T(8,128)(2,1)S(1)}, bf16[768,384]{1,0:T(8,128)(2,1)}, u32[]{:S(2)}) copy-start(bf16[768,384]{1,0:T(8,128)(2,1)} %param.35) | copy-start | bytes 1769476
  81.6 32.9 %copy-start.37 = (f32[768]{0:T(1024)S(1)}, f32[768]{0:T(1024)}, u32[]{:S(2)}) copy-start(f32[768]{0:T(1024)} %param.37) | copy-start | bytes 9220
  85.5 73.1 %all-reduce.10.cloned.1.call-start = ((), (), s32[]{:S(2)}) async-start(), calls=%async_computation.18 | async-start | bytes 1572864 | tf_op jit(solution)/shard_map/psum | solution.py:171
  123.9 34.7 %copy-start.4 = (bf16[256,768]{1,0:T(8,128)(2,1)S(1)}, bf16[256,768]{1,0:T(8,128)(2,1)}, u32[]{:S(2)}) copy-start(bf16[256,768]{1,0:T(8,128)(2,1)} %all-reduce.6.cloned.1.call-done) | copy-start | bytes 1179652
  123.9 34.7 %copy-start.10 = (bf16[1,256,768]{2,1,0:T(8,128)(2,1)S(1)}, bf16[1,256,768]{2,1,0:T(8,128)(2,1)}, u32[]{:S(2)}) copy-start(bf16[1,256,768]{2,1,0:T(8,128)(2,1)} %param.44) | copy-start | bytes 1179652
  123.9 34.7 %copy-start.49 = (f32[256]{0:T(256)S(1)}, f32[256]{0:T(256)}, u32[]{:S(2)}) copy-start(f32[256]{0:T(256)} %copy-done.48) | copy-start | bytes 3076
  123.9 34.7 %copy-start.53 = (f32[256]{0:T(256)S(1)}, f32[256]{0:T(256)}, u32[]{:S(2)}) copy-start(f32[256]{0:T(256)} %copy-done.52) | copy-start | bytes 3076
  123.9 34.8 %copy-start.58 = (f32[768]{0:T(1024)S(1)}, f32[768]{0:T(1024)}, u32[]{:S(2)}) copy-start(f32[768]{0:T(1024)} %param.42) | copy-start | bytes 9220
  124.0 95.0 %reduce-scatter.9.cloned.1.call-start = ((), (), s32[]{:S(2)}) async-start(), calls=%async_computation.9 | async-start | bytes 983040 | tf_op jit(solution)/shard_map/reduce_scatter | solution.py:276
  164.2 82.0 %copy-start.6 = (f32[256,768]{1,0:T(8,128)}, f32[256,768]{1,0:T(8,128)S(1)}, u32[]{:S(2)}) copy-start(f32[256,768]{1,0:T(8,128)S(1)} %fusion.39) | copy-start | bytes 2359300
  195.6 48.2 %reduce-scatter.11.cloned.1.call-start = ((), (), s32[]{:S(2)}) async-start(), calls=%async_computation.10 | async-start | bytes 983040 | tf_op jit(solution)/shard_map/reduce_scatter | solution.py:279
  196.4 75.1 %all-reduce.8.cloned.1.call-start = ((), (), s32[]{:S(2)}) async-start(), calls=%async_computation.11 | async-start | bytes 786432 | tf_op jit(solution)/shard_map/psum | solution.py:310
  246.1 94.0 %reduce-scatter.19.cloned.1.call-start = ((), (), s32[]{:S(2)}) async-start(), calls=%async_computation.15 | async-start | bytes 1253376 | tf_op jit(solution)/shard_map/reduce_scatter | solution.py:316
  247.7 147.9 %reduce-scatter.15.cloned.1.call-start = ((), (), s32[]{:S(2)}) async-start(), calls=%async_computation.13 | async-start | bytes 1253376 | tf_op jit(solution)/shard_map/reduce_scatter | solution.py:314
  249.4 208.1 %reduce-scatter.13.cloned.1.call-start = ((), (), s32[]{:S(2)}) async-start(), calls=%async_computation.12 | async-start | bytes 1253376 | tf_op jit(solution)/shard_map/reduce_scatter | solution.py:313
  251.1 268.1 %reduce-scatter.17.cloned.1.call-start = ((), (), s32[]{:S(2)}) async-start(), calls=%async_computation.14 | async-start | bytes 1253376 | tf_op jit(solution)/shard_map/reduce_scatter | solution.py:315
  252.8 345.8 %reduce-scatter.21.cloned.1.call-start = ((), (), s32[]{:S(2)}) async-start(), calls=%async_computation.16 | async-start | bytes 5013504 | tf_op jit(solution)/shard_map/reduce_scatter | solution.py:317
  256.0 421.7 %reduce-scatter.23.cloned.1.call-start = ((), (), s32[]{:S(2)}) async-start(), calls=%async_computation.17 | async-start | bytes 5013504 | tf_op jit(solution)/shard_map/reduce_scatter | solution.py:318
  263.8 74.3 %copy-start.7 = (f32[256,768]{1,0:T(8,128)S(1)}, f32[256,768]{1,0:T(8,128)}, u32[]{:S(2)}) copy-start(f32[256,768]{1,0:T(8,128)} %copy-done.6) | copy-start | bytes 2359300
  263.8 413.9 %copy-start.1 = (bf16[1536,768]{1,0:T(8,128)(2,1)S(1)}, bf16[1536,768]{1,0:T(8,128)(2,1)}, u32[]{:S(2)}) copy-start(bf16[1536,768]{1,0:T(8,128)(2,1)} %param.41) | copy-start | bytes 7077892
  (50 other events, 345.4 us)
Sparse Core Ops, SparseCore 0:
  85.7 25.7 all-reduce.5
  124.1 34.5 all-reduce.9
  195.7 23.2 reduce-scatter.8
  221.2 22.5 reduce-scatter.10
  246.5 24.9 all-reduce.7
  276.0 58.0 reduce-scatter.18
  338.7 56.8 reduce-scatter.14
  400.3 57.1 reduce-scatter.12
  462.1 57.0 reduce-scatter.16
  524.0 74.5 reduce-scatter.20
  603.0 74.5 reduce-scatter.22
where the time goes:
time: 685 us; the launch traced here: 684 us
  waiting for transfers between devices  437 us (64%)
  blocking collectives  101 us (15%)
  matrix products  66.3 us (10%)
  other arithmetic  45.6 us (7%)
  local copies, waits for them, and re-layouts  17.4 us (3%)
  between operations  15.9 us (2%)
    reduce_scatter x1, waiting for transfers between devices, per_device(): lax.psum_scatter(grad_upw, ('seq', 'batch'), scatter_dimension=0, tiled=T...  79.4 us
    reduce_scatter x1, waiting for transfers between devices, per_device(): lax.psum_scatter(grad_down, ('seq', 'batch'), scatter_dimension=1, tiled=...  79.1 us
    psum x1, blocking collectives, per_device(): lax.psum((jnp.sum(grad_normed_first * unit_first, axis=0), jnp.sum(grad_n...  62.1 us
    reduce_scatter x1, waiting for transfers between devices, per_device(): lax.psum_scatter(grad_queryw, ('seq', 'batch'), scatter_dimension=0, tile...  61.9 us
    reduce_scatter x1, waiting for transfers between devices, per_device(): lax.psum_scatter(grad_valuew, ('seq', 'batch'), scatter_dimension=0, tile...  61.7 us
    reduce_scatter x1, waiting for transfers between devices, per_device(): lax.psum_scatter(grad_keyw, ('seq', 'batch'), scatter_dimension=0, tiled=...  55.5 us
    psum x1, waiting for transfers between devices, per_device(): lax.psum(jnp.dot(active, down_weight, preferred_element_type=jnp.float32)...  31.8 us
    all_gather x1, blocking collectives, per_device(): lax.all_gather(keys, 'seq', axis=0, tiled=True)  21.7 us
  transfers between devices with their start and end apart: 11, of which 10 were waited for; matrix products, arithmetic and copies ran while one was open for 5% of the time, Pallas kernels for 0%

commit v1 on v0

--- a/solution.py
+++ b/solution.py
@@ -1,9 +1,16 @@
+import functools
+from types import SimpleNamespace
+
 import jax
 import jax.numpy as jnp
 from jax import lax
+from jax.experimental import pallas as pl
+from jax.experimental.pallas import tpu as pltpu
 from jax.sharding import PartitionSpec as P
 
 HEAD_DIM = 64
+f32, bf16, i32 = jnp.float32, jnp.bfloat16, jnp.int32
+MESH = pl.DeviceIdType.MESH
 
 
 epsilon = 1e-05
@@ -48,7 +55,644 @@
     return state
 
 
-def per_device(
+def dot(a, b, ca=1, cb=0):
+    return lax.dot_general(a, b, (((ca,), (cb,)), ((), ())), preferred_element_type=f32)
+
+
+def rope_tables(pos, half):
+    index = lax.broadcasted_iota(i32, (half, 1), 0).astype(f32)
+    rates = jnp.exp(-jnp.log(f32(10000.0)) * index / half)
+    angles = rates * pos
+    return jnp.cos(angles), jnp.sin(angles)
+
+
+def rotate_t(lin, cosine, sine):
+    width, rows = lin.shape
+    parts = lin.reshape(width // HEAD_DIM, 2, HEAD_DIM // 2, rows)
+    first, second = parts[:, 0], parts[:, 1]
+    turned = [first * cosine - second * sine, second * cosine + first * sine]
+    return jnp.stack(turned, axis=1).reshape(width, rows)
+
+
+def gelu_both(u):
+    square = u * u
+    t = jnp.tanh(0.7978845608028654 * (u + 0.044715 * square * u))
+    half = 0.5 * (1.0 + t)
+    slope = half + 0.5 * u * (1.0 - t * t) * (0.7978845608028654 * (1.0 + 3 * 0.044715 * square))
+    return u * half, slope
+
+
+def row_chunks(rows, body, size=64):
+    def step(i, _):
+        body(pl.ds(pl.multiple_of(i * size, size), size))
+        return 0
+
+    lax.fori_loop(0, rows // size, step, 0)
+
+
+def folded(rows):
+    total = jnp.sum(rows, axis=0, keepdims=True)
+    return sum(total[:, k : k + 128] for k in range(0, total.shape[1], 128))
+
+
+ROWS, WIDTH, LOCAL, GROUP, HIDDEN, BLOCK = 256, 768, 384, 192, 1536, 48
+
+
+def scratch_spec():
+    vm = pltpu.VMEM
+    heads = (3, HEAD_DIM, ROWS)
+    full32, full16, turned = vm((ROWS, WIDTH), f32), vm((ROWS, WIDTH), bf16), vm((WIDTH, ROWS), bf16)
+
+    def job(columns):
+        return [
+            vm((2, 2, 2, 2, BLOCK, columns), bf16), vm((2, 2, 2, BLOCK, columns), bf16),
+            vm((2, 2, BLOCK, columns), bf16), vm((2, BLOCK, columns), bf16), vm((BLOCK, columns), bf16),
+        ]
+
+    return dict(
+        hist=vm((8, ROWS, WIDTH), bf16), wup=vm((6, WIDTH, 256), bf16), wdown=vm((6, 256, WIDTH), bf16),
+        wof=vm((2, 2, GROUP, WIDTH), bf16),
+        qown=vm((2, *heads), bf16), kown=vm((2, *heads), bf16), vown=vm((2, *heads), bf16),
+        qt=vm((2, *heads), bf16), kt=vm((4, *heads), bf16), vt=vm((4, *heads), bf16),
+        scores=vm((3, 2, 4, ROWS, ROWS), f32), bias=vm((ROWS, ROWS), f32),
+        peak=vm((3, 2, 1, ROWS), f32), denom=vm((3, 2, 1, ROWS), f32), acc=vm((3, 2, HEAD_DIM, ROWS), f32),
+        delta=vm((3, 2, 1, ROWS), f32), cosine=vm((32, ROWS), f32), sine=vm((32, ROWS), f32),
+        mix=vm((2, 2, GROUP, ROWS), bf16), mixout=vm((GROUP, ROWS), bf16),
+        unit1=full32, inv1=vm((ROWS, 1), f32), norm1=full16, norm1t=turned,
+        hidden=full32, attn=full32, unit2=full32, inv2=vm((ROWS, 1), f32), norm2=full16, norm2t=turned,
+        gblock=full32, gmlp=full16, gmlpt=turned, hacc=full32, gact=vm((6, ROWS, 256), f32),
+        act=vm((6, ROWS, 256), bf16), gup=vm((6, ROWS, 256), bf16), gnorm2=full32, gnew=full32, upsum=vm((6, 1, 256), f32),
+        ghid=vm((2, ROWS, WIDTH), bf16), mlp=vm((2, ROWS, WIDTH), bf16), gin=vm((2, ROWS, WIDTH), bf16),
+        dpart=vm((2, 2, GROUP, ROWS), bf16), dsend=vm((2, 2, GROUP, ROWS), bf16), dout=vm((2, *heads), bf16),
+        dkv=vm((4, 2, GROUP, ROWS), bf16), dkvin=vm((4, 2, GROUP, ROWS), bf16),
+        dq=vm((2, 3, HEAD_DIM, ROWS), f32), dqout=vm((GROUP, ROWS), bf16), dqin=vm((GROUP, ROWS), bf16),
+        own0=vm((2, GROUP, ROWS), f32), lin=vm((3, 2, GROUP, ROWS), bf16), gattnt=turned,
+        small=vm((5, 16, WIDTH), f32), smallin=vm((3, 16, WIDTH), f32), smallz=vm((3, 16, WIDTH), f32),
+        job0=job(HIDDEN), job1=job(HIDDEN), job2=job(LOCAL), job3=job(640), job4=job(512),
+        ssem=pltpu.SemaphoreType.DMA((64,)), rsem=pltpu.SemaphoreType.DMA((64,)), lsem=pltpu.SemaphoreType.DMA((16,)),
+    )
+
+
+def layer_kernel(make, *refs):
+    R = make(refs)
+    z, b, y = lax.axis_index("seq"), lax.axis_index("batch"), lax.axis_index("tensor")
+    near, flip, far = z + 1 - 2 * (z % 2), (z + 2) % 4, 3 - z
+    m, p, xbit, core = z % 2, z // 2, b // 2, b % 2
+    to_near, to_flip, to_far = dict(seq=near), dict(seq=flip), dict(seq=far)
+    to_y, to_diag = dict(tensor=1 - y), dict(seq=near, tensor=1 - y)
+    to_x, to_core = dict(batch=(b + 2) % 4), dict(batch=b + 1 - 2 * core)
+    barrier = pltpu.get_barrier_semaphore()
+    everyone = [to_near, to_flip, to_far, to_y, to_diag, to_x, to_core]
+    for there in everyone:
+        pl.semaphore_signal(barrier, inc=1, device_id=there, device_id_type=MESH)
+    started = []
+
+    def send(src, dst, there):
+        i = len(started)
+        copy = pltpu.make_async_remote_copy(
+            src, dst, R.ssem.at[i], R.rsem.at[i], device_id=there, device_id_type=MESH
+        )
+        copy.start()
+        started.append(copy)
+        return copy
+
+    def fetch(src, dst, i):
+        copy = pltpu.make_async_copy(src, dst, R.lsem.at[i])
+        copy.start()
+        return copy
+
+    get_out = fetch(R.wout, R.wof.at[0], 0)
+    get_hist = fetch(R.history, R.hist, 1)
+    get_down = fetch(R.wdown_h, R.wdown, 2)
+    get_up = [fetch(R.wup_h.at[:, pl.ds(256 * n, 256)], R.wup.at[n], 3 + n) for n in range(6)]
+    ends, total = [], 0
+    for i in range(R.windows.shape[0]):
+        total = total + R.windows[i]
+        ends.append(total)
+    base = [R.order[k] * ROWS for k in (z, near, flip, far)]
+    lane = lax.broadcasted_iota(i32, (1, ROWS), 1)
+
+    def norm_first(rows):
+        x = R.x[rows].astype(f32)
+        centred = x - jnp.mean(x, axis=-1, keepdims=True)
+        inverse = lax.rsqrt(jnp.mean(centred * centred, axis=-1, keepdims=True) + epsilon)
+        unit = centred * inverse
+        R.unit1[rows] = unit
+        R.inv1[rows] = inverse
+        R.norm1[rows] = (unit * R.gain1[...] + R.shift1[...]).astype(bf16)
+
+    row_chunks(ROWS, norm_first)
+    cosine, sine = rope_tables((base[0] + lane).astype(f32), HEAD_DIM // 2)
+    R.cosine[...] = cosine
+    R.sine[...] = sine
+    split = (2, 3, HEAD_DIM, ROWS)
+    R.kown[...] = rotate_t(dot(R.norm1[...], R.wk[...]).T, cosine, sine).astype(bf16).reshape(split)
+    pl.semaphore_wait(barrier, len(everyone))
+    k_in = [send(R.kown.at[m], R.kt.at[2], to_flip), send(R.kown.at[1 - m], R.kt.at[3], to_far)]
+    k_in.append(send(R.kown.at[1 - m], R.kt.at[1], to_near))
+    R.vown[...] = dot(R.norm1[...], R.wv[...]).T.astype(bf16).reshape(split)
+    v_in = [send(R.vown.at[m], R.vt.at[2], to_flip), send(R.vown.at[1 - m], R.vt.at[3], to_far)]
+    v_in.append(send(R.vown.at[1 - m], R.vt.at[1], to_near))
+    queries = rotate_t(dot(R.norm1[...], R.wq[...]).T, cosine, sine) * 0.125
+    R.qown[...] = queries.astype(bf16).reshape(split)
+    q_in = send(R.qown.at[1 - m], R.qt.at[1], to_near)
+    get_out.wait()
+    out_in = send(R.wof.at[0], R.wof.at[1], to_y)
+    R.qt[0] = R.qown[m]
+    R.kt[0] = R.kown[m]
+    R.vt[0] = R.vown[m]
+
+    def tile(j, r, first=False):
+        qpos = base[j] + lane
+        start = 0 * qpos
+        for end in ends:
+            start = jnp.maximum(start, jnp.where(qpos >= end, end, 0))
+        kpos = base[r] + lax.broadcasted_iota(i32, (ROWS, ROWS), 0)
+        R.bias[...] = jnp.where((kpos <= qpos) & (kpos >= start), 0.0, -1e30).astype(f32)
+        for h in range(3):
+            s = dot(R.kt[r, h], R.qt[j, h], 0, 0) + R.bias[...]
+            R.scores[h, j, r] = s
+            top = jnp.max(s, axis=0, keepdims=True)
+            if first:
+                e = jnp.exp(s - top)
+                R.denom[h, j] = jnp.sum(e, axis=0, keepdims=True)
+                R.acc[h, j] = dot(R.vt[r, h], e.astype(bf16))
+            else:
+                old = R.peak[h, j]
+                top = jnp.maximum(top, old)
+                e = jnp.exp(s - top)
+                alpha = jnp.exp(old - top)
+                R.denom[h, j] = R.denom[h, j] * alpha + jnp.sum(e, axis=0, keepdims=True)
+                R.acc[h, j] = R.acc[h, j] * alpha + dot(R.vt[r, h], e.astype(bf16))
+            R.peak[h, j] = top
+
+    tile(0, 0, True)
+    R.small[0] = jnp.zeros((16, WIDTH), f32)
+    mix_last = R.mixw[8]
+
+    def block_grads(rows):
+        g = R.cotb[rows].astype(f32) + mix_last * R.cotn[rows].astype(f32)
+        R.gblock[rows] = g
+        low = g.astype(bf16)
+        R.gmlp[rows] = low
+        R.small[0, 4:5] += 0.5 * jnp.sum(low.astype(f32), axis=0, keepdims=True)
+
+    row_chunks(ROWS, block_grads)
+    R.gmlpt[...] = R.gmlp[...].T
+    R.norm1t[...] = R.norm1[...].T
+    for c in (k_in[2], v_in[2], q_in):
+        c.wait_recv()
+    tile(0, 1)
+    tile(1, 1, True)
+    tile(1, 0)
+    get_hist.wait()
+
+    def history_sum(rows):
+        cot = R.cotn[rows].astype(f32)
+        total = 0
+        for j in range(8):
+            h = R.hist[j, rows].astype(f32)
+            total = total + R.mixw[j] * h
+            R.small[0, 5 + j // 6 : 6 + j // 6, 128 * (j % 6) : 128 * (j % 6) + 128] += 0.5 * folded(h * cot)
+        R.hacc[rows] = total
+
+    row_chunks(ROWS, history_sum, 32)
+    get_down.wait()
+
+    def active_grad(n, _):
+        R.gact[n] = dot(R.gmlp[...], R.wdown[n], 1, 1)
+        return 0
+
+    lax.fori_loop(0, 6, active_grad, 0)
+    for c in (k_in[0], v_in[0]):
+        c.wait_recv()
+    tile(1, 2)
+    tile(0, 2)
+    for c in (k_in[1], v_in[1]):
+        c.wait_recv()
+    tile(1, 3)
+
+    def finish(j):
+        for h in range(3):
+            R.acc[h, j] = R.acc[h, j] * (1.0 / R.denom[h, j])
+            R.peak[h, j] = R.peak[h, j] + jnp.log(R.denom[h, j])
+        return jnp.concatenate([R.acc[h, j] for h in range(3)], axis=0).astype(bf16)
+
+    R.mixout[...] = finish(1)
+    mix_in = [send(R.mixout, R.mix.at[1, 1], to_diag), send(R.mixout, R.mix.at[0, 1], to_near)]
+    tile(0, 3)
+    R.mix[0, 0] = finish(0)
+    mix_in.append(send(R.mix.at[0, 0], R.mix.at[1, 0], to_y))
+    for c in get_up:
+        c.wait()
+    out_in.wait_recv()
+    for c in mix_in:
+        c.wait_recv()
+    out = 0
+    for t in range(2):
+        for a in range(2):
+            out = out + dot(R.mix[(t + y) % 2, (a + m) % 2], R.wof[(t + y) % 2, a], 0, 0)
+    R.attn[...] = out
+
+    def norm_second(rows):
+        hidden = R.x[rows].astype(f32) + R.attn[rows]
+        R.hidden[rows] = hidden
+        centred = hidden - jnp.mean(hidden, axis=-1, keepdims=True)
+        inverse = lax.rsqrt(jnp.mean(centred * centred, axis=-1, keepdims=True) + epsilon)
+        unit = centred * inverse
+        R.unit2[rows] = unit
+        R.inv2[rows] = inverse
+        R.norm2[rows] = (unit * R.gain2[...] + R.shift2[...]).astype(bf16)
+
+    row_chunks(ROWS, norm_second)
+
+    def mlp_step(n, _):
+        u = dot(R.norm2[...], R.wup[n]) + R.upb[n]
+        active, slope = gelu_both(u)
+        R.act[n] = active.astype(bf16)
+        grad = (R.gact[n] * slope).astype(bf16)
+        R.gup[n] = grad
+        R.upsum[n] = jnp.sum(grad.astype(f32), axis=0, keepdims=True)
+        back = dot(grad, R.wup[n], 1, 1)
+
+        @pl.when(n == 0)
+        def _():
+            R.gnorm2[...] = back
+
+        @pl.when(n > 0)
+        def _():
+            R.gnorm2[...] += back
+
+        return 0
+
+    lax.fori_loop(0, 6, mlp_step, 0)
+
+    def norm_back(grad, unit, inverse, gain):
+        scaled = grad * gain
+        return inverse * (
+            scaled
+            - jnp.mean(scaled, axis=-1, keepdims=True)
+            - unit * jnp.mean(scaled * unit, axis=-1, keepdims=True)
+        )
+
+    def second_back(rows):
+        back = norm_back(R.gnorm2[rows], R.unit2[rows], R.inv2[rows], R.gain2[...])
+        R.ghid[0, rows] = (0.5 * R.gblock[rows] + back).astype(bf16)
+
+    row_chunks(ROWS, second_back)
+    for t in (1, 0):
+        for a in (1, 0):
+            part = dot(R.wof[t, (a + m) % 2], R.ghid[0], 1, 1).astype(bf16)
+            if t == 0 and a == 0:
+                R.dpart[0, 0] = part
+            else:
+                R.dsend[t, a] = part
+    d_in = [
+        send(R.dsend.at[1, 1], R.dpart.at[1, 1], to_diag),
+        send(R.dsend.at[1, 0], R.dpart.at[0, 1], to_y),
+        send(R.dsend.at[0, 1], R.dpart.at[1, 0], to_near),
+    ]
+    ghid_in = send(R.ghid.at[0], R.ghid.at[1], to_y)
+
+    bits = dict(core=core, x=xbit, near=m, flip=p)
+    where = dict(core=to_core, x=to_x, near=to_near, flip=to_flip)
+    place = dict(core=0, x=1, near=2, flip=3)
+
+    class Job:
+        def __init__(self, bufs, route):
+            self.grads, self.landing, self.route, self.copy, self.step = bufs[0], bufs[1:], route, None, 0
+
+        def put(self, value, columns):
+            for k in range(16):
+                at = tuple((k >> place[axis]) & 1 for axis in self.route)
+                self.grads[(*at, slice(None), columns)] = value[BLOCK * k : BLOCK * k + BLOCK].astype(bf16)
+
+        def mine(self):
+            return tuple(bits[axis] for axis in self.route[: self.step])
+
+        def push(self):
+            axis = self.route[self.step]
+            self.copy = send(self.grads.at[(*self.mine(), 1 - bits[axis])], self.landing[self.step], where[axis])
+
+        def pull(self, out=None):
+            self.copy.wait_recv()
+            landing = self.landing[self.step]
+            self.step += 1
+            kept = self.mine()
+            left = 4 - self.step
+
+            def add(i, _):
+                at = tuple((i // 2**k) % 2 for k in range(left))
+                both = self.grads[(*kept, *at)].astype(f32) + landing[at if at else Ellipsis].astype(f32)
+                if out is None:
+                    self.grads[(*kept, *at)] = both.astype(bf16)
+                else:
+                    out[...] = both
+                return 0
+
+            if left:
+                lax.fori_loop(0, 2**left, add, 0)
+            else:
+                add(0, 0)
+
+        def turn(self):
+            self.pull()
+            self.push()
+
+    usual = tuple(dict(core=0, x=0, near=0, flip=0))
+    x_last = tuple(dict(core=0, near=0, flip=0, x=0))
+    job_down, job_up = Job(R.job0, usual), Job(R.job1, usual)
+    job_out, job_a, job_b = Job(R.job2, usual), Job(R.job3, usual), Job(R.job4, x_last)
+
+    def wide(job, left, right):
+        def step(n, _):
+            job.put(dot(left[...], right[n]), pl.ds(pl.multiple_of(256 * n, 256), 256))
+            return 0
+
+        lax.fori_loop(0, 6, step, 0)
+
+    wide(job_down, R.gmlpt, R.act)
+    job_down.push()
+    R.norm2t[...] = R.norm2[...].T
+    wide(job_up, R.norm2t, R.gup)
+    job_up.push()
+
+    R.gnew[...] = jnp.zeros((ROWS, WIDTH), f32)
+
+    def down_step(n, _):
+        R.gnew[...] += dot(R.act[n], R.wdown[n])
+        return 0
+
+    lax.fori_loop(0, 6, down_step, 0)
+    R.mlp[0] = R.gnew[...].astype(bf16)
+    mlp_in = send(R.mlp.at[0], R.mlp.at[1], to_y)
+    job_down.turn()
+
+    for c in d_in:
+        c.wait_recv()
+    for j in range(2):
+        both = R.dpart[j, 0].astype(f32) + R.dpart[j, 1].astype(f32)
+        R.dout[j] = both.astype(bf16).reshape(3, HEAD_DIM, ROWS)
+        for h in range(3):
+            R.delta[h, j] = jnp.sum(R.dout[j, h].astype(f32) * R.acc[h, j], axis=0, keepdims=True)
+
+    def back_block(r, first):
+        for h in range(3):
+            dk, dv = 0, 0
+            for j in range(2):
+                probs = jnp.exp(R.scores[h, j, r] - R.peak[h, j])
+                grad = dot(R.vt[r, h], R.dout[j, h], 0, 0)
+                low = (probs * (grad - R.delta[h, j])).astype(bf16)
+                dv = dv + dot(R.dout[j, h], probs.astype(bf16), 1, 1)
+                dk = dk + dot(R.qt[j, h], low, 1, 1)
+                dq = dot(R.kt[r, h], low)
+                R.dq[j, h] = dq if first else R.dq[j, h] + dq
+            at = pl.ds(HEAD_DIM * h, HEAD_DIM)
+            if r:
+                R.dkv[r, 0, at] = dk.astype(bf16)
+                R.dkv[r, 1, at] = dv.astype(bf16)
+            else:
+                R.own0[0, at] = dk
+                R.own0[1, at] = dv
+
+    back_block(2, True)
+    kv_in = [send(R.dkv.at[2], R.dkvin.at[2], to_flip)]
+    back_block(3, False)
+    kv_in.append(send(R.dkv.at[3], R.dkvin.at[3], to_far))
+    back_block(1, False)
+    kv_in.append(send(R.dkv.at[1], R.dkvin.at[1], to_near))
+    back_block(0, False)
+    R.dqout[...] = (0.125 * R.dq[1].reshape(GROUP, ROWS)).astype(bf16)
+    dq_in = send(R.dqout, R.dqin, to_near)
+    job_up.turn()
+
+    mlp_in.wait_recv()
+    ghid_in.wait_recv()
+
+    def block_out(rows):
+        both = R.mlp[0, rows].astype(f32) + R.mlp[1, rows].astype(f32) + R.downb[...]
+        value = R.hidden[rows] + both
+        R.o_block[rows] = value.astype(bf16)
+        R.o_next[rows] = (R.hacc[rows] + mix_last * value).astype(bf16)
+        attn = R.attn[rows]
+        for k, term in enumerate((value * R.cotn[rows].astype(f32), value * value, attn * attn, both * both)):
+            R.small[0, 6:7, 128 * (2 + k) : 128 * (3 + k)] += 0.5 * folded(term)
+        hid = R.ghid[0, rows].astype(f32) + R.ghid[1, rows].astype(f32)
+        R.gblock[rows] = hid
+        R.gmlp[rows] = hid.astype(bf16)
+        back = R.gnorm2[rows]
+        R.small[0, 2:3] += jnp.sum(back * R.unit2[rows], axis=0, keepdims=True)
+        R.small[0, 3:4] += jnp.sum(back, axis=0, keepdims=True)
+
+    row_chunks(ROWS, block_out, 32)
+    for n in range(6):
+        R.small[0, 8 + n // 3 : 9 + n // 3, 256 * (n % 3) : 256 * (n % 3) + 256] = R.upsum[n]
+    R.gattnt[...] = R.gmlp[...].T
+    mixed = jnp.concatenate([R.mix[0, (a + m) % 2] for a in range(2)], axis=0)
+    job_out.put(dot(R.gattnt[...], mixed, 1, 1), slice(None))
+    job_out.push()
+    job_out.turn()
+
+    for c in (*kv_in, dq_in):
+        c.wait_recv()
+    cosine, sine = R.cosine[...], -R.sine[...]
+    for k in range(2):
+        ours = R.own0[k] + R.dkvin[2, k].astype(f32)
+        theirs = R.dkvin[1, k].astype(f32) + R.dkvin[3, k].astype(f32)
+        if k == 0:
+            ours, theirs = rotate_t(ours, cosine, sine), rotate_t(theirs, cosine, sine)
+        R.lin[1 + k, m] = ours.astype(bf16)
+        R.lin[1 + k, 1 - m] = theirs.astype(bf16)
+    R.lin[0, m] = rotate_t(0.125 * R.dq[0].reshape(GROUP, ROWS), cosine, sine).astype(bf16)
+    R.lin[0, 1 - m] = rotate_t(R.dqin[...].astype(f32), cosine, sine).astype(bf16)
+    lins = [R.lin[k].reshape(LOCAL, ROWS) for k in range(3)]
+    first = dot(R.wq[...], lins[0]) + dot(R.wk[...], lins[1]) + dot(R.wv[...], lins[2])
+    R.gnew[...] = first.T
+
+    def first_back(rows):
+        grad = R.gnew[rows]
+        R.gin[0, rows] = norm_back(grad, R.unit1[rows], R.inv1[rows], R.gain1[...]).astype(bf16)
+        R.small[0, 0:1] += jnp.sum(grad * R.unit1[rows], axis=0, keepdims=True)
+        R.small[0, 1:2] += jnp.sum(grad, axis=0, keepdims=True)
+
+    row_chunks(ROWS, first_back)
+    gin_in = send(R.gin.at[0], R.gin.at[1], to_y)
+    small_in = send(R.small.at[0, pl.ds(0, 8)], R.smallin.at[0, pl.ds(0, 8)], to_y)
+    every = jnp.concatenate(lins, axis=0)
+    job_a.put(dot(R.norm1t[...], every[:640], 1, 1), slice(None))
+    job_a.push()
+    job_b.put(dot(R.norm1t[...], every[640:], 1, 1), slice(None))
+    job_b.push()
+    job_a.turn()
+    job_b.turn()
+    small_in.wait_recv()
+    R.small[1, 0:8] = R.small[0, 0:8] + R.smallin[0, 0:8]
+    R.small[1, 8:16] = R.small[0, 8:16]
+    small_in = send(R.small.at[1], R.smallin.at[1], to_core)
+    job_down.turn()
+    job_up.turn()
+    small_in.wait_recv()
+    R.small[2] = R.small[1] + R.smallin[1]
+    small_in = send(R.small.at[2], R.smallin.at[2], to_x)
+    job_out.turn()
+    small_in.wait_recv()
+    R.small[3] = R.small[2] + R.smallin[2]
+    small_in = [
+        send(R.small.at[3], R.smallz.at[k], there) for k, there in enumerate((to_near, to_flip, to_far))
+    ]
+    job_down.turn()
+    job_up.turn()
+    job_out.turn()
+    job_a.turn()
+    job_b.turn()
+    job_a.turn()
+    job_b.turn()
+    gin_in.wait_recv()
+
+    def grad_in(rows):
+        both = R.gin[0, rows].astype(f32) + R.gin[1, rows].astype(f32)
+        R.o_gin[rows] = (R.gblock[rows] + both).astype(bf16)
+
+    row_chunks(ROWS, grad_in)
+    for c in small_in:
+        c.wait_recv()
+    R.o_small[...] = (R.small[3] + R.smallz[0]) + (R.smallz[1] + R.smallz[2])
+    job_down.pull(R.o_down)
+    job_up.pull(R.o_up)
+    job_out.pull(R.o_out)
+    job_a.pull(R.o_a)
+    job_b.pull(R.o_b)
+    for c in started:
+        c.wait_send()
+
+
+def last_kernel(make, *refs):
+    R = make(refs)
+    R.next[0] = R.o_next[...]
+    R.block[0] = R.o_block[...]
+    R.gin[0] = R.o_gin[...]
+
+    def history_back(rows):
+        cot = R.cotn[rows].astype(f32)
+        for j in range(8):
+            R.ghist[j, 0, rows] = (R.mixw[j] * cot).astype(bf16)
+
+    row_chunks(ROWS, history_back)
+    R.gq[...] = R.o_a[:, :LOCAL]
+    R.gk[...] = jnp.concatenate([R.o_a[:, LOCAL:], R.o_b[:, :128]], axis=1)
+    R.gv[...] = R.o_b[:, 128:]
+    R.gup[...] = R.o_up[...]
+    R.gout[...] = R.o_out[...].T
+    R.gdown[...] = R.o_down[...].T
+    for i, ref in enumerate((R.gain1, R.shift1, R.gain2, R.shift2, R.downb)):
+        ref[...] = R.o_small[i]
+    R.upb[0:WIDTH] = R.o_small[8]
+    R.upb[WIDTH:HIDDEN] = R.o_small[9]
+    parts = [R.o_small[5 + k // 6 : 6 + k // 6, 128 * (k % 6) : 128 * (k % 6) + 128] for k in range(12)]
+    sums = jnp.sum(jnp.concatenate(parts, axis=0), axis=1, keepdims=True)
+    row = jnp.broadcast_to(sums, (12, 128)).T[0:1]
+    R.sums[...] = row
+
+
+def out_spec(shape, dtype=f32):
+    return jax.ShapeDtypeStruct(shape, dtype)
+
+
+def namer(*groups):
+    names = [name for group in groups for name in group]
+    return lambda refs: SimpleNamespace(**dict(zip(names, refs)))
+
+
+def per_device_block(
+    inputs,
+    history,
+    window_lengths,
+    block_order,
+    first_gain,
+    first_shift,
+    query_weight,
+    key_weight,
+    value_weight,
+    out_weight,
+    second_gain,
+    second_shift,
+    up_weight,
+    up_bias,
+    down_weight,
+    down_bias,
+    mix_weights,
+    cotangent_next,
+    cotangent_block,
+):
+    vmem, hbm, smem = (pl.BlockSpec(memory_space=s) for s in (pltpu.VMEM, pl.ANY, pltpu.SMEM))
+    args = dict(
+        x=inputs[0], cotn=cotangent_next[0], cotb=cotangent_block[0],
+        wq=query_weight, wk=key_weight, wv=value_weight,
+        gain1=first_gain[None], shift1=first_shift[None], gain2=second_gain[None], shift2=second_shift[None],
+        upb=up_bias.reshape(6, 1, 256), downb=down_bias[None],
+        wout=out_weight.reshape(2, GROUP, WIDTH), history=history[:, 0], wup_h=up_weight,
+        wdown_h=down_weight.reshape(6, 256, WIDTH),
+        windows=window_lengths[0], order=block_order, mixw=mix_weights,
+    )
+    specs = [vmem] * 12 + [hbm] * 4 + [smem] * 3
+    outs = dict(
+        o_next=out_spec((ROWS, WIDTH), bf16), o_block=out_spec((ROWS, WIDTH), bf16), o_gin=out_spec((ROWS, WIDTH), bf16),
+        o_down=out_spec((BLOCK, HIDDEN)), o_up=out_spec((BLOCK, HIDDEN)), o_out=out_spec((BLOCK, LOCAL)),
+        o_a=out_spec((BLOCK, 640)), o_b=out_spec((BLOCK, 512)), o_small=out_spec((16, WIDTH)),
+    )
+    scratch = scratch_spec()
+    tree = jax.tree.structure(scratch)
+    flat, names = [], []
+    for name, spec in scratch.items():
+        several = isinstance(spec, list)
+        names.append((name, len(spec) if several else 0))
+        flat.extend(spec if several else [spec])
+
+    def make(refs):
+        R, k = dict(zip([*args, *outs], refs)), len(args) + len(outs)
+        for name, count in names:
+            R[name] = refs[k : k + count] if count else refs[k]
+            k += max(count, 1)
+        return SimpleNamespace(**R)
+
+    held = pl.pallas_call(
+        functools.partial(layer_kernel, make),
+        out_shape=list(outs.values()),
+        in_specs=specs,
+        out_specs=[vmem] * len(outs),
+        scratch_shapes=flat,
+        compiler_params=pltpu.CompilerParams(
+            collective_id=1, has_side_effects=True, vmem_limit_bytes=63 * 2**20
+        ),
+    )(*args.values())
+    held = dict(zip(outs, held))
+    rows3 = (1, ROWS, WIDTH)
+    results = dict(
+        next=out_spec(rows3, bf16), block=out_spec(rows3, bf16), gin=out_spec(rows3, bf16),
+        ghist=out_spec((8, *rows3), bf16), gain1=out_spec((WIDTH,)), shift1=out_spec((WIDTH,)),
+        gq=out_spec((BLOCK, LOCAL)), gk=out_spec((BLOCK, LOCAL)), gv=out_spec((BLOCK, LOCAL)),
+        gout=out_spec((LOCAL, BLOCK)), gain2=out_spec((WIDTH,)), shift2=out_spec((WIDTH,)),
+        gup=out_spec((BLOCK, HIDDEN)), upb=out_spec((HIDDEN,)), gdown=out_spec((HIDDEN, BLOCK)),
+        downb=out_spec((WIDTH,)), sums=out_spec((1, 12)),
+    )
+    given = dict(cotn=cotangent_next[0], mixw=mix_weights, **held)
+    done = pl.pallas_call(
+        functools.partial(last_kernel, namer(given, results)),
+        out_shape=list(results.values()),
+        in_specs=[vmem, smem] + [vmem] * len(held),
+        out_specs=[vmem] * len(results),
+        compiler_params=pltpu.CompilerParams(vmem_limit_bytes=40 * 2**20),
+    )(*given.values())
+    sums = done[-1][0]
+    entries = float(lax.axis_size("batch") * lax.axis_size("seq") * ROWS * WIDTH)
+    return (*done[:-1], sums[:9], jnp.sqrt(sums[9:12] / entries))
+
+
+def device_function(mesh):
+    return per_device_block if mesh.shape["seq"] == 4 else per_device_general
+
+
+def per_device_general(
     inputs,
     history,
     window_lengths,
@@ -404,5 +1048,5 @@
         P(),
     )
     return jax.shard_map(
-        per_device, mesh=mesh, in_specs=in_specs, out_specs=out_specs, check_vma=False
-    )
+        device_function(mesh), mesh=mesh, in_specs=in_specs, out_specs=out_specs, check_vma=False
+    )

time: 685 us -> 147 us (0.21)
  the two profiles are of different devices: /device:TPU:0 before, /device:TPU:4 now
where the time goes in v1:
time: 147 us
  Pallas kernels  127 us (86%)
  local copies, waits for them, and re-layouts  18.2 us (12%)
    pallas_call x1, Pallas kernels, per_device_block(): pl.pallas_call(functools.partial(layer_kernel, make), out_shape=list(outs...  124 us
    unnamed x24, local copies, waits for them, and re-layouts  10.1 us
    pallas_call x1, Pallas kernels, per_device_block(): pl.pallas_call(functools.partial(last_kernel, namer(given, results)), out...  3.21 us

profile of v1, /device:TPU:4, one launch (start us, length us, event | category | flops | bytes accessed | tf_op | source)
XLA Modules:
  0.0 146.6 jit_solution(3435871619079678191)
XLA Ops:
  0.7 1.3 broadcast_in_dim.15.refs_6_
  1.9 1.3 broadcast_in_dim.16.refs_7_
  3.2 1.3 broadcast_in_dim.17.refs_8_
  4.5 1.3 broadcast_in_dim.18.refs_9_
  5.7 1.3 broadcast_in_dim.19.refs_11_
  7.0 1.3 reshape.50.refs_10_
  8.3 123.9 %shard_map.322 = (bf16[256,768]{1,0:T(8,128)(2,1)}, bf16[256,768]{1,0:T(8,128)(2,1)}, bf16[256,768]{1,0:T(8,128)(2,1)}, f32[48,1536]{1,0:T(8,128)}, f32[48,1536]...) custom-call(bf16[256,768]{1,0:T(8,128)(2,1)} %bitcast.16, ...), custom_call_target="tpu_custom_call" | custom-call | tf_op jit(solution)/shard_map/pallas_call | solution.py:658
  132.2 0.0 copy-done
  132.2 0.0 copy-done.10
  132.2 0.0 copy-start.1
  132.2 1.0 copy-done.1
  133.2 1.0 copy-done.2
  134.2 1.0 copy-done.3
  135.2 1.0 copy-done.4
  136.2 1.0 copy-done.5
  137.1 0.9 copy-done.6
  138.0 0.9 copy-done.7
  138.9 0.9 copy-done.8
  139.8 0.8 copy-done.9
  140.6 3.2 %shard_map.323 = (bf16[1,256,768]{2,1,0:T(8,128)(2,1)}, bf16[1,256,768]{2,1,0:T(8,128)(2,1)}, bf16[1,256,768]{2,1,0:T(8,128)(2,1)}, bf16[8,1,256,768]{3,2,1,0:T(...) custom-call(bf16[256,768]{1,0:T(8,128)(2,1)S(1)} %bitcast.12, ...), custom_call_target="tpu_custom_call" | custom-call | tf_op jit(solution)/shard_map/pallas_call | solution.py:679
  143.8 0.6 sqrt_bitcast_fusion
  144.4 0.5 slice_bitcast_fusion
  144.9 0.7 copy.37
  145.7 1.0 copy.38
  (10 shorter events, 0.0 us)
Async XLA Ops:
  8.3 123.9 %copy-start = (bf16[1,256,768]{2,1,0:T(8,128)(2,1)S(1)}, bf16[1,256,768]{2,1,0:T(8,128)(2,1)}, u32[]{:S(2)}) copy-start(bf16[1,256,768]{2,1,0:T(8,128)(2,1)} %param.36) | copy-start | bytes 1179652
  8.3 123.9 %copy-start.10 = (f32[9]{0:T(128)S(1)}, f32[9]{0:T(128)}, u32[]{:S(2)}) copy-start(f32[9]{0:T(128)} %refs_1_.1) | copy-start | bytes 112
  132.2 1.0 copy-start.1
  133.2 1.0 copy-start.2
  134.2 1.0 copy-start.3
  135.2 1.0 copy-start.4
  136.2 1.0 copy-start.5
  137.1 0.9 copy-start.6
  138.0 0.9 copy-start.7
  138.9 0.9 copy-start.8
  139.8 0.8 copy-start.9

commit v2 on v1

--- a/solution.py
+++ b/solution.py
@@ -110,26 +110,28 @@
         ]
 
     return dict(
-        hist=vm((8, ROWS, WIDTH), bf16), wup=vm((6, WIDTH, 256), bf16), wdown=vm((6, 256, WIDTH), bf16),
-        wof=vm((2, 2, GROUP, WIDTH), bf16),
-        qown=vm((2, *heads), bf16), kown=vm((2, *heads), bf16), vown=vm((2, *heads), bf16),
-        qt=vm((2, *heads), bf16), kt=vm((4, *heads), bf16), vt=vm((4, *heads), bf16),
-        scores=vm((3, 2, 4, ROWS, ROWS), f32), bias=vm((ROWS, ROWS), f32),
+        cotn=full16, cotb=full16, wq=vm((WIDTH, LOCAL), bf16), wk=vm((WIDTH, LOCAL), bf16), wv=vm((WIDTH, LOCAL), bf16),
+        hist=vm((8, ROWS, WIDTH), bf16), wup=vm((WIDTH, HIDDEN), bf16), wdown=vm((HIDDEN, WIDTH), bf16),
+        wof=vm((2, 2, 3, HEAD_DIM, WIDTH), bf16),
+        vectors=vm((5, 1, WIDTH), f32), upb=vm((1, HIDDEN), f32), upsum=vm((1, HIDDEN), f32),
+        qown=vm((2, *heads), bf16), kvown=vm((2, 3, 2, HEAD_DIM, ROWS), bf16),
+        qt=vm((2, *heads), bf16), kv=vm((4, 3, 2, HEAD_DIM, ROWS), bf16),
+        scores=vm((3, 2, 4, ROWS, ROWS), f32), bias=vm((2, 4, ROWS, ROWS), f32),
         peak=vm((3, 2, 1, ROWS), f32), denom=vm((3, 2, 1, ROWS), f32), acc=vm((3, 2, HEAD_DIM, ROWS), f32),
         delta=vm((3, 2, 1, ROWS), f32), cosine=vm((32, ROWS), f32), sine=vm((32, ROWS), f32),
-        mix=vm((2, 2, GROUP, ROWS), bf16), mixout=vm((GROUP, ROWS), bf16),
+        mix=vm((2, 2, *heads), bf16), mixout=vm(heads, bf16),
         unit1=full32, inv1=vm((ROWS, 1), f32), norm1=full16, norm1t=turned,
         hidden=full32, attn=full32, unit2=full32, inv2=vm((ROWS, 1), f32), norm2=full16, norm2t=turned,
-        gblock=full32, gmlp=full16, gmlpt=turned, hacc=full32, gact=vm((6, ROWS, 256), f32),
-        act=vm((6, ROWS, 256), bf16), gup=vm((6, ROWS, 256), bf16), gnorm2=full32, gnew=full32, upsum=vm((6, 1, 256), f32),
+        gblock=full32, gmlp=full16, gmlpt=turned, hacc=full32, gact=vm((ROWS, HIDDEN), f32),
+        act=vm((ROWS, HIDDEN), bf16), gup=vm((ROWS, HIDDEN), bf16), gnorm2=full32, gnew=full32,
         ghid=vm((2, ROWS, WIDTH), bf16), mlp=vm((2, ROWS, WIDTH), bf16), gin=vm((2, ROWS, WIDTH), bf16),
-        dpart=vm((2, 2, GROUP, ROWS), bf16), dsend=vm((2, 2, GROUP, ROWS), bf16), dout=vm((2, *heads), bf16),
-        dkv=vm((4, 2, GROUP, ROWS), bf16), dkvin=vm((4, 2, GROUP, ROWS), bf16),
-        dq=vm((2, 3, HEAD_DIM, ROWS), f32), dqout=vm((GROUP, ROWS), bf16), dqin=vm((GROUP, ROWS), bf16),
-        own0=vm((2, GROUP, ROWS), f32), lin=vm((3, 2, GROUP, ROWS), bf16), gattnt=turned,
+        dpart=vm((2, 2, *heads), bf16), dsend=vm((2, 2, *heads), bf16), dout=vm((2, *heads), bf16),
+        dkv=vm((4, 3, 2, HEAD_DIM, ROWS), bf16), dkvin=vm((4, 3, 2, HEAD_DIM, ROWS), bf16),
+        dq=vm((3, HEAD_DIM, ROWS), f32), dqout=vm(heads, bf16), dqin=vm(heads, bf16),
+        own0=vm((3, 2, HEAD_DIM, ROWS), f32), lin=vm((3, 2, *heads), bf16), gattnt=turned,
         small=vm((5, 16, WIDTH), f32), smallin=vm((3, 16, WIDTH), f32), smallz=vm((3, 16, WIDTH), f32),
         job0=job(HIDDEN), job1=job(HIDDEN), job2=job(LOCAL), job3=job(640), job4=job(512),
-        ssem=pltpu.SemaphoreType.DMA((64,)), rsem=pltpu.SemaphoreType.DMA((64,)), lsem=pltpu.SemaphoreType.DMA((16,)),
+        ssem=pltpu.SemaphoreType.DMA((96,)), rsem=pltpu.SemaphoreType.DMA((96,)), lsem=pltpu.SemaphoreType.DMA((16,)),
     )
 
 
@@ -161,14 +163,22 @@
         copy.start()
         return copy
 
-    get_out = fetch(R.wout, R.wof.at[0], 0)
-    get_hist = fetch(R.history, R.hist, 1)
-    get_down = fetch(R.wdown_h, R.wdown, 2)
-    get_up = [fetch(R.wup_h.at[:, pl.ds(256 * n, 256)], R.wup.at[n], 3 + n) for n in range(6)]
+    get_q = fetch(R.wq_h, R.wq, 0)
+    get_k = fetch(R.wk_h, R.wk, 1)
+    get_v = fetch(R.wv_h, R.wv, 2)
+    get_cot = [fetch(R.cotn_h, R.cotn, 3), fetch(R.cotb_h, R.cotb, 4)]
+    get_out = fetch(R.wout, R.wof.at[0], 5)
+    get_hist = fetch(R.history, R.hist, 6)
+    get_down = fetch(R.wdown_h, R.wdown, 7)
+    get_up = fetch(R.wup_h, R.wup, 8)
     ends, total = [], 0
     for i in range(R.windows.shape[0]):
         total = total + R.windows[i]
         ends.append(total)
+    for i, ref in enumerate((R.gain1_in, R.shift1_in, R.gain2_in, R.shift2_in, R.downb_in)):
+        R.vectors[i] = ref[...][None]
+    R.upb[...] = R.upb_in[...][None]
+    R.gain1, R.shift1, R.gain2, R.shift2, R.downb = (R.vectors.at[i] for i in range(5))
     base = [R.order[k] * ROWS for k in (z, near, flip, far)]
     lane = lax.broadcasted_iota(i32, (1, ROWS), 1)
 
@@ -186,47 +196,42 @@
     R.cosine[...] = cosine
     R.sine[...] = sine
     split = (2, 3, HEAD_DIM, ROWS)
-    R.kown[...] = rotate_t(dot(R.norm1[...], R.wk[...]).T, cosine, sine).astype(bf16).reshape(split)
+    get_k.wait()
+    R.kvown[:, :, 0] = rotate_t(dot(R.norm1[...], R.wk[...]).T, cosine, sine).astype(bf16).reshape(split)
+    get_v.wait()
+    R.kvown[:, :, 1] = dot(R.norm1[...], R.wv[...]).T.astype(bf16).reshape(split)
     pl.semaphore_wait(barrier, len(everyone))
-    k_in = [send(R.kown.at[m], R.kt.at[2], to_flip), send(R.kown.at[1 - m], R.kt.at[3], to_far)]
-    k_in.append(send(R.kown.at[1 - m], R.kt.at[1], to_near))
-    R.vown[...] = dot(R.norm1[...], R.wv[...]).T.astype(bf16).reshape(split)
-    v_in = [send(R.vown.at[m], R.vt.at[2], to_flip), send(R.vown.at[1 - m], R.vt.at[3], to_far)]
-    v_in.append(send(R.vown.at[1 - m], R.vt.at[1], to_near))
+    near_in, flip_in, far_in = [], [], []
+
+    def kv_out(h):
+        near_in.append(send(R.kvown.at[1 - m, h], R.kv.at[1, h], to_near))
+        flip_in.append(send(R.kvown.at[m, h], R.kv.at[2, h], to_flip))
+        far_in.append(send(R.kvown.at[1 - m, h], R.kv.at[3, h], to_far))
+
+    kv_out(0)
+    get_q.wait()
     queries = rotate_t(dot(R.norm1[...], R.wq[...]).T, cosine, sine) * 0.125
     R.qown[...] = queries.astype(bf16).reshape(split)
-    q_in = send(R.qown.at[1 - m], R.qt.at[1], to_near)
+    q_in = [send(R.qown.at[1 - m, h], R.qt.at[1, h], to_near) for h in range(1)]
+    kv_out(1)
+    q_in.append(send(R.qown.at[1 - m, 1], R.qt.at[1, 1], to_near))
+    kv_out(2)
+    q_in.append(send(R.qown.at[1 - m, 2], R.qt.at[1, 2], to_near))
     get_out.wait()
     out_in = send(R.wof.at[0], R.wof.at[1], to_y)
     R.qt[0] = R.qown[m]
-    R.kt[0] = R.kown[m]
-    R.vt[0] = R.vown[m]
-
-    def tile(j, r, first=False):
+    R.kv[0] = R.kvown[m]
+
+    for j in range(2):
         qpos = base[j] + lane
         start = 0 * qpos
         for end in ends:
             start = jnp.maximum(start, jnp.where(qpos >= end, end, 0))
-        kpos = base[r] + lax.broadcasted_iota(i32, (ROWS, ROWS), 0)
-        R.bias[...] = jnp.where((kpos <= qpos) & (kpos >= start), 0.0, -1e30).astype(f32)
-        for h in range(3):
-            s = dot(R.kt[r, h], R.qt[j, h], 0, 0) + R.bias[...]
-            R.scores[h, j, r] = s
-            top = jnp.max(s, axis=0, keepdims=True)
-            if first:
-                e = jnp.exp(s - top)
-                R.denom[h, j] = jnp.sum(e, axis=0, keepdims=True)
-                R.acc[h, j] = dot(R.vt[r, h], e.astype(bf16))
-            else:
-                old = R.peak[h, j]
-                top = jnp.maximum(top, old)
-                e = jnp.exp(s - top)
-                alpha = jnp.exp(old - top)
-                R.denom[h, j] = R.denom[h, j] * alpha + jnp.sum(e, axis=0, keepdims=True)
-                R.acc[h, j] = R.acc[h, j] * alpha + dot(R.vt[r, h], e.astype(bf16))
-            R.peak[h, j] = top
-
-    tile(0, 0, True)
+        for r in range(4):
+            kpos = base[r] + lax.broadcasted_iota(i32, (ROWS, ROWS), 0)
+            R.bias[j, r] = jnp.where((kpos <= qpos) & (kpos >= start), 0.0, -1e30).astype(f32)
+    for c in get_cot:
+        c.wait()
     R.small[0] = jnp.zeros((16, WIDTH), f32)
     mix_last = R.mixw[8]
 
@@ -240,11 +245,6 @@
     row_chunks(ROWS, block_grads)
     R.gmlpt[...] = R.gmlp[...].T
     R.norm1t[...] = R.norm1[...].T
-    for c in (k_in[2], v_in[2], q_in):
-        c.wait_recv()
-    tile(0, 1)
-    tile(1, 1, True)
-    tile(1, 0)
     get_hist.wait()
 
     def history_sum(rows):
@@ -260,38 +260,64 @@
     get_down.wait()
 
     def active_grad(n, _):
-        R.gact[n] = dot(R.gmlp[...], R.wdown[n], 1, 1)
+        at = pl.ds(pl.multiple_of(256 * n, 256), 256)
+        R.gact[:, at] = dot(R.gmlp[...], R.wdown[at], 1, 1)
         return 0
 
     lax.fori_loop(0, 6, active_grad, 0)
-    for c in (k_in[0], v_in[0]):
-        c.wait_recv()
-    tile(1, 2)
-    tile(0, 2)
-    for c in (k_in[1], v_in[1]):
-        c.wait_recv()
-    tile(1, 3)
-
-    def finish(j):
-        for h in range(3):
-            R.acc[h, j] = R.acc[h, j] * (1.0 / R.denom[h, j])
-            R.peak[h, j] = R.peak[h, j] + jnp.log(R.denom[h, j])
-        return jnp.concatenate([R.acc[h, j] for h in range(3)], axis=0).astype(bf16)
-
-    R.mixout[...] = finish(1)
-    mix_in = [send(R.mixout, R.mix.at[1, 1], to_diag), send(R.mixout, R.mix.at[0, 1], to_near)]
-    tile(0, 3)
-    R.mix[0, 0] = finish(0)
-    mix_in.append(send(R.mix.at[0, 0], R.mix.at[1, 0], to_y))
-    for c in get_up:
-        c.wait()
+
+    def tile(h, j, r, first=False):
+        s = dot(R.kv[r, h, 0], R.qt[j, h], 0, 0) + R.bias[j, r]
+        R.scores[h, j, r] = s
+        top = jnp.max(s, axis=0, keepdims=True)
+        if first:
+            e = jnp.exp(s - top)
+            R.denom[h, j] = jnp.sum(e, axis=0, keepdims=True)
+            R.acc[h, j] = dot(R.kv[r, h, 1], e.astype(bf16))
+        else:
+            old = R.peak[h, j]
+            top = jnp.maximum(top, old)
+            e = jnp.exp(s - top)
+            alpha = jnp.exp(old - top)
+            R.denom[h, j] = R.denom[h, j] * alpha + jnp.sum(e, axis=0, keepdims=True)
+            R.acc[h, j] = R.acc[h, j] * alpha + dot(R.kv[r, h, 1], e.astype(bf16))
+        R.peak[h, j] = top
+
+    def finish(h, j):
+        R.acc[h, j] = R.acc[h, j] * (1.0 / R.denom[h, j])
+        R.peak[h, j] = R.peak[h, j] + jnp.log(R.denom[h, j])
+        return R.acc[h, j].astype(bf16)
+
+    mix_in = []
+    for h in range(3):
+        tile(h, 0, 0, True)
+    for h in range(3):
+        near_in[h].wait_recv()
+        q_in[h].wait_recv()
+        tile(h, 0, 1)
+        tile(h, 1, 1, True)
+        tile(h, 1, 0)
+        flip_in[h].wait_recv()
+        tile(h, 1, 2)
+        tile(h, 0, 2)
+        far_in[h].wait_recv()
+        tile(h, 1, 3)
+        tile(h, 0, 3)
+        R.mixout[h] = finish(h, 1)
+        R.mix[0, 0, h] = finish(h, 0)
+        mix_in.append(send(R.mixout.at[h], R.mix.at[1, 1, h], to_diag))
+        mix_in.append(send(R.mix.at[0, 0, h], R.mix.at[1, 0, h], to_y))
+        mix_in.append(send(R.mixout.at[h], R.mix.at[0, 1, h], to_near))
+    get_up.wait()
     out_in.wait_recv()
     for c in mix_in:
         c.wait_recv()
+    group = (GROUP, ROWS)
     out = 0
     for t in range(2):
         for a in range(2):
-            out = out + dot(R.mix[(t + y) % 2, (a + m) % 2], R.wof[(t + y) % 2, a], 0, 0)
+            side = R.mix[(t + y) % 2, (a + m) % 2].reshape(group)
+            out = out + dot(side, R.wof[(t + y) % 2, a].reshape(GROUP, WIDTH), 0, 0)
     R.attn[...] = out
 
     def norm_second(rows):
@@ -305,27 +331,17 @@
         R.norm2[rows] = (unit * R.gain2[...] + R.shift2[...]).astype(bf16)
 
     row_chunks(ROWS, norm_second)
-
-    def mlp_step(n, _):
-        u = dot(R.norm2[...], R.wup[n]) + R.upb[n]
+    for n in range(6):
+        at = slice(256 * n, 256 * n + 256)
+        u = dot(R.norm2[...], R.wup[:, at]) + R.upb[:, at]
         active, slope = gelu_both(u)
-        R.act[n] = active.astype(bf16)
-        grad = (R.gact[n] * slope).astype(bf16)
-        R.gup[n] = grad
-        R.upsum[n] = jnp.sum(grad.astype(f32), axis=0, keepdims=True)
-        back = dot(grad, R.wup[n], 1, 1)
-
-        @pl.when(n == 0)
-        def _():
-            R.gnorm2[...] = back
-
-        @pl.when(n > 0)
-        def _():
-            R.gnorm2[...] += back
-
-        return 0
-
-    lax.fori_loop(0, 6, mlp_step, 0)
+        R.act[:, at] = active.astype(bf16)
+        grad = (R.gact[:, at] * slope).astype(bf16)
+        R.gup[:, at] = grad
+        R.upsum[:, at] = jnp.sum(grad.astype(f32), axis=0, keepdims=True)
+        if n == 2:
+            R.gnorm2[...] = dot(R.gup[:, :WIDTH], R.wup[:, :WIDTH], 1, 1)
+    R.gnorm2[...] += dot(R.gup[:, WIDTH:], R.wup[:, WIDTH:], 1, 1)
 
     def norm_back(grad, unit, inverse, gain):
         scaled = grad * gain
@@ -340,18 +356,21 @@
         R.ghid[0, rows] = (0.5 * R.gblock[rows] + back).astype(bf16)
 
     row_chunks(ROWS, second_back)
-    for t in (1, 0):
-        for a in (1, 0):
-            part = dot(R.wof[t, (a + m) % 2], R.ghid[0], 1, 1).astype(bf16)
-            if t == 0 and a == 0:
-                R.dpart[0, 0] = part
-            else:
-                R.dsend[t, a] = part
-    d_in = [
-        send(R.dsend.at[1, 1], R.dpart.at[1, 1], to_diag),
-        send(R.dsend.at[1, 0], R.dpart.at[0, 1], to_y),
-        send(R.dsend.at[0, 1], R.dpart.at[1, 0], to_near),
-    ]
+    d_in = []
+    order = [(1, 1), (1, 0), (0, 1), (0, 0)]
+    for h in range(3):
+        weights = jnp.concatenate([R.wof[t, (a + m) % 2, h] for t, a in order], axis=0)
+        parts = dot(weights, R.ghid[0], 1, 1).astype(bf16).reshape(4, HEAD_DIM, ROWS)
+        for k in range(3):
+            R.dsend[(*order[k], h)] = parts[k]
+        R.dpart[0, 0, h] = parts[3]
+        d_in.append(
+            [
+                send(R.dsend.at[1, 1, h], R.dpart.at[1, 1, h], to_diag),
+                send(R.dsend.at[1, 0, h], R.dpart.at[0, 1, h], to_y),
+                send(R.dsend.at[0, 1, h], R.dpart.at[1, 0, h], to_near),
+            ]
+        )
     ghid_in = send(R.ghid.at[0], R.ghid.at[1], to_y)
 
     bits = dict(core=core, x=xbit, near=m, flip=p)
@@ -383,11 +402,11 @@
 
             def add(i, _):
                 at = tuple((i // 2**k) % 2 for k in range(left))
-                both = self.grads[(*kept, *at)].astype(f32) + landing[at if at else Ellipsis].astype(f32)
+                mine, theirs = self.grads[(*kept, *at)], landing[at if at else Ellipsis]
                 if out is None:
-                    self.grads[(*kept, *at)] = both.astype(bf16)
+                    self.grads[(*kept, *at)] = mine + theirs
                 else:
-                    out[...] = both
+                    out[...] = mine.astype(f32) + theirs.astype(f32)
                 return 0
 
             if left:
@@ -399,75 +418,81 @@
             self.pull()
             self.push()
 
-    usual = tuple(dict(core=0, x=0, near=0, flip=0))
-    x_last = tuple(dict(core=0, near=0, flip=0, x=0))
+    usual = tuple(place)
     job_down, job_up = Job(R.job0, usual), Job(R.job1, usual)
-    job_out, job_a, job_b = Job(R.job2, usual), Job(R.job3, usual), Job(R.job4, x_last)
+    job_out, job_a, job_b = Job(R.job2, usual), Job(R.job3, usual), Job(R.job4, usual)
 
     def wide(job, left, right):
         def step(n, _):
-            job.put(dot(left[...], right[n]), pl.ds(pl.multiple_of(256 * n, 256), 256))
+            at = pl.ds(pl.multiple_of(256 * n, 256), 256)
+            job.put(dot(left[...], right[:, at]), at)
             return 0
 
         lax.fori_loop(0, 6, step, 0)
 
     wide(job_down, R.gmlpt, R.act)
     job_down.push()
+
+    kv_in, dq_in = [], []
+
+    def back_head(h):
+        for c in d_in[h]:
+            c.wait_recv()
+        for j in range(2):
+            both = R.dpart[j, 0, h].astype(f32) + R.dpart[j, 1, h].astype(f32)
+            R.dout[j, h] = both.astype(bf16)
+            R.delta[h, j] = jnp.sum(R.dout[j, h].astype(f32) * R.acc[h, j], axis=0, keepdims=True)
+        total = [0, 0]
+        for r in (2, 3, 1, 0):
+            dk, dv = 0, 0
+            for j in range(2):
+                probs = jnp.exp(R.scores[h, j, r] - R.peak[h, j])
+                grad = dot(R.kv[r, h, 1], R.dout[j, h], 0, 0)
+                low = (probs * (grad - R.delta[h, j])).astype(bf16)
+                dv = dv + dot(R.dout[j, h], probs.astype(bf16), 1, 1)
+                dk = dk + dot(R.qt[j, h], low, 1, 1)
+                total[j] = total[j] + dot(R.kv[r, h, 0], low)
+            if r:
+                R.dkv[r, h, 0] = dk.astype(bf16)
+                R.dkv[r, h, 1] = dv.astype(bf16)
+                kv_in.append(send(R.dkv.at[r, h], R.dkvin.at[r, h], (to_near, to_flip, to_far)[r - 1]))
+            else:
+                R.own0[h, 0] = dk
+                R.own0[h, 1] = dv
+        R.dqout[h] = (0.125 * total[1]).astype(bf16)
+        dq_in.append(send(R.dqout.at[h], R.dqin.at[h], to_near))
+        R.dq[h] = 0.125 * total[0]
+
+    back_head(0)
+    job_down.turn()
+    back_head(1)
+    back_head(2)
     R.norm2t[...] = R.norm2[...].T
     wide(job_up, R.norm2t, R.gup)
     job_up.push()
-
-    R.gnew[...] = jnp.zeros((ROWS, WIDTH), f32)
-
-    def down_step(n, _):
-        R.gnew[...] += dot(R.act[n], R.wdown[n])
-        return 0
-
-    lax.fori_loop(0, 6, down_step, 0)
-    R.mlp[0] = R.gnew[...].astype(bf16)
+    R.mlp[0] = dot(R.act[...], R.wdown[...]).astype(bf16)
     mlp_in = send(R.mlp.at[0], R.mlp.at[1], to_y)
+    job_up.turn()
+
+    ghid_in.wait_recv()
+
+    def whole_hidden(rows):
+        hid = R.ghid[0, rows].astype(f32) + R.ghid[1, rows].astype(f32)
+        R.gblock[rows] = hid
+        R.gmlp[rows] = hid.astype(bf16)
+        back = R.gnorm2[rows]
+        R.small[0, 2:3] += jnp.sum(back * R.unit2[rows], axis=0, keepdims=True)
+        R.small[0, 3:4] += jnp.sum(back, axis=0, keepdims=True)
+
+    row_chunks(ROWS, whole_hidden)
+    R.gattnt[...] = R.gmlp[...].T
+    mixed = jnp.concatenate([R.mix[0, (a + m) % 2].reshape(group) for a in range(2)], axis=0)
+    job_out.put(dot(R.gattnt[...], mixed, 1, 1), slice(None))
+    job_out.push()
+    job_out.turn()
     job_down.turn()
 
-    for c in d_in:
-        c.wait_recv()
-    for j in range(2):
-        both = R.dpart[j, 0].astype(f32) + R.dpart[j, 1].astype(f32)
-        R.dout[j] = both.astype(bf16).reshape(3, HEAD_DIM, ROWS)
-        for h in range(3):
-            R.delta[h, j] = jnp.sum(R.dout[j, h].astype(f32) * R.acc[h, j], axis=0, keepdims=True)
-
-    def back_block(r, first):
-        for h in range(3):
-            dk, dv = 0, 0
-            for j in range(2):
-                probs = jnp.exp(R.scores[h, j, r] - R.peak[h, j])
-                grad = dot(R.vt[r, h], R.dout[j, h], 0, 0)
-                low = (probs * (grad - R.delta[h, j])).astype(bf16)
-                dv = dv + dot(R.dout[j, h], probs.astype(bf16), 1, 1)
-                dk = dk + dot(R.qt[j, h], low, 1, 1)
-                dq = dot(R.kt[r, h], low)
-                R.dq[j, h] = dq if first else R.dq[j, h] + dq
-            at = pl.ds(HEAD_DIM * h, HEAD_DIM)
-            if r:
-                R.dkv[r, 0, at] = dk.astype(bf16)
-                R.dkv[r, 1, at] = dv.astype(bf16)
-            else:
-                R.own0[0, at] = dk
-                R.own0[1, at] = dv
-
-    back_block(2, True)
-    kv_in = [send(R.dkv.at[2], R.dkvin.at[2], to_flip)]
-    back_block(3, False)
-    kv_in.append(send(R.dkv.at[3], R.dkvin.at[3], to_far))
-    back_block(1, False)
-    kv_in.append(send(R.dkv.at[1], R.dkvin.at[1], to_near))
-    back_block(0, False)
-    R.dqout[...] = (0.125 * R.dq[1].reshape(GROUP, ROWS)).astype(bf16)
-    dq_in = send(R.dqout, R.dqin, to_near)
-    job_up.turn()
-
     mlp_in.wait_recv()
-    ghid_in.wait_recv()
 
     def block_out(rows):
         both = R.mlp[0, rows].astype(f32) + R.mlp[1, rows].astype(f32) + R.downb[...]
@@ -477,34 +502,24 @@
         attn = R.attn[rows]
         for k, term in enumerate((value * R.cotn[rows].astype(f32), value * value, attn * attn, both * both)):
             R.small[0, 6:7, 128 * (2 + k) : 128 * (3 + k)] += 0.5 * folded(term)
-        hid = R.ghid[0, rows].astype(f32) + R.ghid[1, rows].astype(f32)
-        R.gblock[rows] = hid
-        R.gmlp[rows] = hid.astype(bf16)
-        back = R.gnorm2[rows]
-        R.small[0, 2:3] += jnp.sum(back * R.unit2[rows], axis=0, keepdims=True)
-        R.small[0, 3:4] += jnp.sum(back, axis=0, keepdims=True)
 
     row_chunks(ROWS, block_out, 32)
-    for n in range(6):
-        R.small[0, 8 + n // 3 : 9 + n // 3, 256 * (n % 3) : 256 * (n % 3) + 256] = R.upsum[n]
-    R.gattnt[...] = R.gmlp[...].T
-    mixed = jnp.concatenate([R.mix[0, (a + m) % 2] for a in range(2)], axis=0)
-    job_out.put(dot(R.gattnt[...], mixed, 1, 1), slice(None))
-    job_out.push()
-    job_out.turn()
-
-    for c in (*kv_in, dq_in):
-        c.wait_recv()
+    R.small[0, 8:9] = R.upsum[:, :WIDTH]
+    R.small[0, 9:10] = R.upsum[:, WIDTH:]
+
     cosine, sine = R.cosine[...], -R.sine[...]
-    for k in range(2):
-        ours = R.own0[k] + R.dkvin[2, k].astype(f32)
-        theirs = R.dkvin[1, k].astype(f32) + R.dkvin[3, k].astype(f32)
-        if k == 0:
-            ours, theirs = rotate_t(ours, cosine, sine), rotate_t(theirs, cosine, sine)
-        R.lin[1 + k, m] = ours.astype(bf16)
-        R.lin[1 + k, 1 - m] = theirs.astype(bf16)
-    R.lin[0, m] = rotate_t(0.125 * R.dq[0].reshape(GROUP, ROWS), cosine, sine).astype(bf16)
-    R.lin[0, 1 - m] = rotate_t(R.dqin[...].astype(f32), cosine, sine).astype(bf16)
+    for h in range(3):
+        for c in (*kv_in[3 * h : 3 * h + 3], dq_in[h]):
+            c.wait_recv()
+        for k in range(2):
+            ours = R.own0[h, k] + R.dkvin[2, h, k].astype(f32)
+            theirs = R.dkvin[1, h, k].astype(f32) + R.dkvin[3, h, k].astype(f32)
+            if k == 0:
+                ours, theirs = rotate_t(ours, cosine, sine), rotate_t(theirs, cosine, sine)
+            R.lin[1 + k, m, h] = ours.astype(bf16)
+            R.lin[1 + k, 1 - m, h] = theirs.astype(bf16)
+        R.lin[0, m, h] = rotate_t(R.dq[h], cosine, sine).astype(bf16)
+        R.lin[0, 1 - m, h] = rotate_t(R.dqin[h].astype(f32), cosine, sine).astype(bf16)
     lins = [R.lin[k].reshape(LOCAL, ROWS) for k in range(3)]
     first = dot(R.wq[...], lins[0]) + dot(R.wk[...], lins[1]) + dot(R.wv[...], lins[2])
     R.gnew[...] = first.T
@@ -516,15 +531,13 @@
         R.small[0, 1:2] += jnp.sum(grad, axis=0, keepdims=True)
 
     row_chunks(ROWS, first_back)
+    small_in = send(R.small.at[0, pl.ds(0, 8)], R.smallin.at[0, pl.ds(0, 8)], to_y)
     gin_in = send(R.gin.at[0], R.gin.at[1], to_y)
-    small_in = send(R.small.at[0, pl.ds(0, 8)], R.smallin.at[0, pl.ds(0, 8)], to_y)
     every = jnp.concatenate(lins, axis=0)
     job_a.put(dot(R.norm1t[...], every[:640], 1, 1), slice(None))
     job_a.push()
     job_b.put(dot(R.norm1t[...], every[640:], 1, 1), slice(None))
     job_b.push()
-    job_a.turn()
-    job_b.turn()
     small_in.wait_recv()
     R.small[1, 0:8] = R.small[0, 0:8] + R.smallin[0, 0:8]
     R.small[1, 8:16] = R.small[0, 8:16]
@@ -534,17 +547,17 @@
     small_in.wait_recv()
     R.small[2] = R.small[1] + R.smallin[1]
     small_in = send(R.small.at[2], R.smallin.at[2], to_x)
+    job_a.turn()
+    job_b.turn()
     job_out.turn()
     small_in.wait_recv()
     R.small[3] = R.small[2] + R.smallin[2]
     small_in = [
         send(R.small.at[3], R.smallz.at[k], there) for k, there in enumerate((to_near, to_flip, to_far))
     ]
-    job_down.turn()
     job_up.turn()
     job_out.turn()
-    job_a.turn()
-    job_b.turn()
+    job_down.pull(R.o_down)
     job_a.turn()
     job_b.turn()
     gin_in.wait_recv()
@@ -554,10 +567,11 @@
         R.o_gin[rows] = (R.gblock[rows] + both).astype(bf16)
 
     row_chunks(ROWS, grad_in)
+    job_a.turn()
+    job_b.turn()
     for c in small_in:
         c.wait_recv()
     R.o_small[...] = (R.small[3] + R.smallz[0]) + (R.smallz[1] + R.smallz[2])
-    job_down.pull(R.o_down)
     job_up.pull(R.o_up)
     job_out.pull(R.o_out)
     job_a.pull(R.o_a)
@@ -566,7 +580,7 @@
         c.wait_send()
 
 
-def last_kernel(make, *refs):
+def last_kernel(make, entries, *refs):
     R = make(refs)
     R.next[0] = R.o_next[...]
     R.block[0] = R.o_block[...]
@@ -582,8 +596,8 @@
     R.gk[...] = jnp.concatenate([R.o_a[:, LOCAL:], R.o_b[:, :128]], axis=1)
     R.gv[...] = R.o_b[:, 128:]
     R.gup[...] = R.o_up[...]
-    R.gout[...] = R.o_out[...].T
-    R.gdown[...] = R.o_down[...].T
+    R.gout[...] = R.o_out[...]
+    R.gdown[...] = R.o_down[...]
     for i, ref in enumerate((R.gain1, R.shift1, R.gain2, R.shift2, R.downb)):
         ref[...] = R.o_small[i]
     R.upb[0:WIDTH] = R.o_small[8]
@@ -591,7 +605,8 @@
     parts = [R.o_small[5 + k // 6 : 6 + k // 6, 128 * (k % 6) : 128 * (k % 6) + 128] for k in range(12)]
     sums = jnp.sum(jnp.concatenate(parts, axis=0), axis=1, keepdims=True)
     row = jnp.broadcast_to(sums, (12, 128)).T[0:1]
-    R.sums[...] = row
+    R.gmix[...] = row[0, :9]
+    R.rms[...] = jnp.sqrt(row / entries)[0, 9:]
 
 
 def out_spec(shape, dtype=f32):
@@ -626,22 +641,19 @@
 ):
     vmem, hbm, smem = (pl.BlockSpec(memory_space=s) for s in (pltpu.VMEM, pl.ANY, pltpu.SMEM))
     args = dict(
-        x=inputs[0], cotn=cotangent_next[0], cotb=cotangent_block[0],
-        wq=query_weight, wk=key_weight, wv=value_weight,
-        gain1=first_gain[None], shift1=first_shift[None], gain2=second_gain[None], shift2=second_shift[None],
-        upb=up_bias.reshape(6, 1, 256), downb=down_bias[None],
-        wout=out_weight.reshape(2, GROUP, WIDTH), history=history[:, 0], wup_h=up_weight,
-        wdown_h=down_weight.reshape(6, 256, WIDTH),
+        x=inputs[0], gain1_in=first_gain, shift1_in=first_shift, gain2_in=second_gain, shift2_in=second_shift,
+        upb_in=up_bias, downb_in=down_bias,
+        cotn_h=cotangent_next[0], cotb_h=cotangent_block[0], wq_h=query_weight, wk_h=key_weight, wv_h=value_weight,
+        wout=out_weight.reshape(2, 3, HEAD_DIM, WIDTH), history=history[:, 0], wup_h=up_weight, wdown_h=down_weight,
         windows=window_lengths[0], order=block_order, mixw=mix_weights,
     )
-    specs = [vmem] * 12 + [hbm] * 4 + [smem] * 3
+    specs = [vmem] * 7 + [hbm] * 9 + [smem] * 3
     outs = dict(
         o_next=out_spec((ROWS, WIDTH), bf16), o_block=out_spec((ROWS, WIDTH), bf16), o_gin=out_spec((ROWS, WIDTH), bf16),
         o_down=out_spec((BLOCK, HIDDEN)), o_up=out_spec((BLOCK, HIDDEN)), o_out=out_spec((BLOCK, LOCAL)),
         o_a=out_spec((BLOCK, 640)), o_b=out_spec((BLOCK, 512)), o_small=out_spec((16, WIDTH)),
     )
     scratch = scratch_spec()
-    tree = jax.tree.structure(scratch)
     flat, names = [], []
     for name, spec in scratch.items():
         several = isinstance(spec, list)
@@ -671,21 +683,22 @@
         next=out_spec(rows3, bf16), block=out_spec(rows3, bf16), gin=out_spec(rows3, bf16),
         ghist=out_spec((8, *rows3), bf16), gain1=out_spec((WIDTH,)), shift1=out_spec((WIDTH,)),
         gq=out_spec((BLOCK, LOCAL)), gk=out_spec((BLOCK, LOCAL)), gv=out_spec((BLOCK, LOCAL)),
-        gout=out_spec((LOCAL, BLOCK)), gain2=out_spec((WIDTH,)), shift2=out_spec((WIDTH,)),
-        gup=out_spec((BLOCK, HIDDEN)), upb=out_spec((HIDDEN,)), gdown=out_spec((HIDDEN, BLOCK)),
-        downb=out_spec((WIDTH,)), sums=out_spec((1, 12)),
-    )
+        gout=out_spec((BLOCK, LOCAL)), gain2=out_spec((WIDTH,)), shift2=out_spec((WIDTH,)),
+        gup=out_spec((BLOCK, HIDDEN)), upb=out_spec((HIDDEN,)), gdown=out_spec((BLOCK, HIDDEN)),
+        downb=out_spec((WIDTH,)), gmix=out_spec((9,)), rms=out_spec((3,)),
+    )
+    entries = float(lax.axis_size("batch") * lax.axis_size("seq") * ROWS * WIDTH)
     given = dict(cotn=cotangent_next[0], mixw=mix_weights, **held)
     done = pl.pallas_call(
-        functools.partial(last_kernel, namer(given, results)),
+        functools.partial(last_kernel, namer(given, results), entries),
         out_shape=list(results.values()),
         in_specs=[vmem, smem] + [vmem] * len(held),
         out_specs=[vmem] * len(results),
-        compiler_params=pltpu.CompilerParams(vmem_limit_bytes=40 * 2**20),
+        compiler_params=pltpu.CompilerParams(vmem_limit_bytes=63 * 2**20),
     )(*given.values())
-    sums = done[-1][0]
-    entries = float(lax.axis_size("batch") * lax.axis_size("seq") * ROWS * WIDTH)
-    return (*done[:-1], sums[:9], jnp.sqrt(sums[9:12] / entries))
+    done = dict(zip(results, done))
+    turned = dict(gout=done[list(results)[9]].T, gdown=done[list(results)[14]].T)
+    return tuple((done | turned).values())
 
 
 def device_function(mesh):

time: 147 us -> 104 us (0.71)
  the two profiles are of different devices: /device:TPU:4 before, /device:TPU:0 now
where the time goes in v2:
time: 104 us; the launch traced here: 103 us
  Pallas kernels  103 us (99%)
    pallas_call x1, Pallas kernels, per_device_block(): pl.pallas_call(functools.partial(layer_kernel, make), out_shape=list(outs...  98.3 us
    pallas_call x1, Pallas kernels, per_device_block(): pl.pallas_call(functools.partial(last_kernel, namer(given, results), entr...  4.36 us

profile of v2, /device:TPU:0, one launch (start us, length us, event | category | flops | bytes accessed | tf_op | source)
XLA Modules:
  0.0 103.4 jit_solution(5462400558486817728)
XLA Ops:
  0.7 98.3 %shard_map.322 = (bf16[256,768]{1,0:T(8,128)(2,1)}, bf16[256,768]{1,0:T(8,128)(2,1)}, bf16[256,768]{1,0:T(8,128)(2,1)}, f32[48,1536]{1,0:T(8,128)}, f32[48,1536]...) custom-call(bf16[256,768]{1,0:T(8,128)(2,1)} %bitcast.12, ...), custom_call_target="tpu_custom_call" | custom-call | tf_op jit(solution)/shard_map/pallas_call | solution.py:670
  98.9 4.4 %shard_map.323 = (bf16[1,256,768]{2,1,0:T(8,128)(2,1)}, bf16[1,256,768]{2,1,0:T(8,128)(2,1)}, bf16[1,256,768]{2,1,0:T(8,128)(2,1)}, bf16[8,1,256,768]{3,2,1,0:T(...) custom-call(bf16[256,768]{1,0:T(8,128)(2,1)} %bitcast.10, ...), custom_call_target="tpu_custom_call" | custom-call | tf_op jit(solution)/shard_map/pallas_call | solution.py:692

commit v3 on v2

--- a/solution.py
+++ b/solution.py
@@ -98,7 +98,7 @@
 ROWS, WIDTH, LOCAL, GROUP, HIDDEN, BLOCK = 256, 768, 384, 192, 1536, 48
 
 
-def scratch_spec():
+def scratch_spec(windows):
     vm = pltpu.VMEM
     heads = (3, HEAD_DIM, ROWS)
     full32, full16, turned = vm((ROWS, WIDTH), f32), vm((ROWS, WIDTH), bf16), vm((WIDTH, ROWS), bf16)
@@ -110,6 +110,8 @@
         ]
 
     return dict(
+        x=full16, gain1_v=vm((WIDTH,), f32), shift1_v=vm((WIDTH,), f32), gain2_v=vm((WIDTH,), f32), shift2_v=vm((WIDTH,), f32),
+        downb_v=vm((WIDTH,), f32), upb_v=vm((HIDDEN,), f32), order=pltpu.SMEM((4,), i32), windows=pltpu.SMEM((windows,), i32), mixw=pltpu.SMEM((9,), f32),
         cotn=full16, cotb=full16, wq=vm((WIDTH, LOCAL), bf16), wk=vm((WIDTH, LOCAL), bf16), wv=vm((WIDTH, LOCAL), bf16),
         hist=vm((8, ROWS, WIDTH), bf16), wup=vm((WIDTH, HIDDEN), bf16), wdown=vm((HIDDEN, WIDTH), bf16),
         wof=vm((2, 2, 3, HEAD_DIM, WIDTH), bf16),
@@ -130,8 +132,11 @@
         dq=vm((3, HEAD_DIM, ROWS), f32), dqout=vm(heads, bf16), dqin=vm(heads, bf16),
         own0=vm((3, 2, HEAD_DIM, ROWS), f32), lin=vm((3, 2, *heads), bf16), gattnt=turned,
         small=vm((5, 16, WIDTH), f32), smallin=vm((3, 16, WIDTH), f32), smallz=vm((3, 16, WIDTH), f32),
-        job0=job(HIDDEN), job1=job(HIDDEN), job2=job(LOCAL), job3=job(640), job4=job(512),
-        ssem=pltpu.SemaphoreType.DMA((96,)), rsem=pltpu.SemaphoreType.DMA((96,)), lsem=pltpu.SemaphoreType.DMA((16,)),
+        job0=job(WIDTH), job1=job(WIDTH), job2=job(WIDTH), job3=job(WIDTH), job4=job(LOCAL), job5=job(640), job6=job(512),
+        s_next=full16, s_block=full16, s_gin=full16, s_down=vm((BLOCK, HIDDEN), f32), s_up=vm((BLOCK, HIDDEN), f32),
+        s_out=vm((BLOCK, LOCAL), f32), s_a=vm((BLOCK, 640), f32), s_b=vm((BLOCK, 512), f32), s_small=vm((16, WIDTH), f32),
+        osem=pltpu.SemaphoreType.DMA((12,)),
+        ssem=pltpu.SemaphoreType.DMA((96,)), rsem=pltpu.SemaphoreType.DMA((96,)), lsem=pltpu.SemaphoreType.DMA((24,)),
     )
 
 
@@ -163,21 +168,31 @@
         copy.start()
         return copy
 
+    get_small = [fetch(R.x_h, R.x, 9)]
+    get_k = fetch(R.wk_h, R.wk, 1)
+    pairs = [(R.gain1_in, R.gain1_v), (R.shift1_in, R.shift1_v), (R.order_in, R.order), (R.windows_in, R.windows)]
+    pairs += [(R.gain2_in, R.gain2_v), (R.shift2_in, R.shift2_v), (R.downb_in, R.downb_v), (R.upb_in, R.upb_v)]
+    pairs.append((R.mixw_in, R.mixw))
+    for i, (src, dst) in enumerate(pairs):
+        get_small.append(fetch(src, dst, 10 + i))
     get_q = fetch(R.wq_h, R.wq, 0)
-    get_k = fetch(R.wk_h, R.wk, 1)
     get_v = fetch(R.wv_h, R.wv, 2)
-    get_cot = [fetch(R.cotn_h, R.cotn, 3), fetch(R.cotb_h, R.cotb, 4)]
-    get_out = fetch(R.wout, R.wof.at[0], 5)
-    get_hist = fetch(R.history, R.hist, 6)
-    get_down = fetch(R.wdown_h, R.wdown, 7)
-    get_up = fetch(R.wup_h, R.wup, 8)
+    written = []
+
+    def write(src, dst):
+        copy = pltpu.make_async_copy(src, dst, R.osem.at[len(written)])
+        copy.start()
+        written.append(copy)
+
+    for c in get_small:
+        c.wait()
     ends, total = [], 0
     for i in range(R.windows.shape[0]):
         total = total + R.windows[i]
         ends.append(total)
-    for i, ref in enumerate((R.gain1_in, R.shift1_in, R.gain2_in, R.shift2_in, R.downb_in)):
+    for i, ref in enumerate((R.gain1_v, R.shift1_v, R.gain2_v, R.shift2_v, R.downb_v)):
         R.vectors[i] = ref[...][None]
-    R.upb[...] = R.upb_in[...][None]
+    R.upb[...] = R.upb_v[...][None]
     R.gain1, R.shift1, R.gain2, R.shift2, R.downb = (R.vectors.at[i] for i in range(5))
     base = [R.order[k] * ROWS for k in (z, near, flip, far)]
     lane = lax.broadcasted_iota(i32, (1, ROWS), 1)
@@ -210,6 +225,11 @@
 
     kv_out(0)
     get_q.wait()
+    get_out = fetch(R.wout, R.wof.at[0], 5)
+    get_cot = [fetch(R.cotn_h, R.cotn, 3), fetch(R.cotb_h, R.cotb, 4)]
+    get_hist = fetch(R.history, R.hist, 6)
+    get_down = fetch(R.wdown_h, R.wdown, 7)
+    get_up = fetch(R.wup_h, R.wup, 8)
     queries = rotate_t(dot(R.norm1[...], R.wq[...]).T, cosine, sine) * 0.125
     R.qown[...] = queries.astype(bf16).reshape(split)
     q_in = [send(R.qown.at[1 - m, h], R.qt.at[1, h], to_near) for h in range(1)]
@@ -330,6 +350,55 @@
         R.inv2[rows] = inverse
         R.norm2[rows] = (unit * R.gain2[...] + R.shift2[...]).astype(bf16)
 
+    bits = dict(core=core, x=xbit, near=m, flip=p)
+    where = dict(core=to_core, x=to_x, near=to_near, flip=to_flip)
+    place = dict(core=0, x=1, near=2, flip=3)
+
+    class Job:
+        def __init__(self, bufs, route):
+            self.grads, self.landing, self.route, self.copy, self.step = bufs[0], bufs[1:], route, None, 0
+
+        def put(self, value, columns):
+            for k in range(16):
+                at = tuple((k >> place[axis]) & 1 for axis in self.route)
+                self.grads[(*at, slice(None), columns)] = value[BLOCK * k : BLOCK * k + BLOCK].astype(bf16)
+
+        def mine(self):
+            return tuple(bits[axis] for axis in self.route[: self.step])
+
+        def push(self):
+            axis = self.route[self.step]
+            self.copy = send(self.grads.at[(*self.mine(), 1 - bits[axis])], self.landing[self.step], where[axis])
+
+        def pull(self, out=None):
+            self.copy.wait_recv()
+            landing = self.landing[self.step]
+            self.step += 1
+            kept = self.mine()
+            left = 4 - self.step
+
+            def add(i, _):
+                at = tuple((i // 2**k) % 2 for k in range(left))
+                mine, theirs = self.grads[(*kept, *at)], landing[at if at else Ellipsis]
+                if out is None:
+                    self.grads[(*kept, *at)] = mine + theirs
+                else:
+                    out[...] = mine.astype(f32) + theirs.astype(f32)
+                return 0
+
+            if left:
+                lax.fori_loop(0, 2**left, add, 0)
+            else:
+                add(0, 0)
+
+        def turn(self):
+            self.pull()
+            self.push()
+
+    usual = tuple(place)
+    down0, down1, up0, up1 = (Job(bufs, usual) for bufs in (R.job0, R.job1, R.job2, R.job3))
+    job_out, job_a, job_b = (Job(bufs, usual) for bufs in (R.job4, R.job5, R.job6))
+
     row_chunks(ROWS, norm_second)
     for n in range(6):
         at = slice(256 * n, 256 * n + 256)
@@ -339,8 +408,12 @@
         grad = (R.gact[:, at] * slope).astype(bf16)
         R.gup[:, at] = grad
         R.upsum[:, at] = jnp.sum(grad.astype(f32), axis=0, keepdims=True)
+        third = slice(256 * (n % 3), 256 * (n % 3) + 256)
+        (down0, down1)[n // 3].put(dot(R.gmlpt[...], R.act[:, at]), third)
         if n == 2:
+            down0.push()
             R.gnorm2[...] = dot(R.gup[:, :WIDTH], R.wup[:, :WIDTH], 1, 1)
+    down1.push()
     R.gnorm2[...] += dot(R.gup[:, WIDTH:], R.wup[:, WIDTH:], 1, 1)
 
     def norm_back(grad, unit, inverse, gain):
@@ -372,66 +445,6 @@
             ]
         )
     ghid_in = send(R.ghid.at[0], R.ghid.at[1], to_y)
-
-    bits = dict(core=core, x=xbit, near=m, flip=p)
-    where = dict(core=to_core, x=to_x, near=to_near, flip=to_flip)
-    place = dict(core=0, x=1, near=2, flip=3)
-
-    class Job:
-        def __init__(self, bufs, route):
-            self.grads, self.landing, self.route, self.copy, self.step = bufs[0], bufs[1:], route, None, 0
-
-        def put(self, value, columns):
-            for k in range(16):
-                at = tuple((k >> place[axis]) & 1 for axis in self.route)
-                self.grads[(*at, slice(None), columns)] = value[BLOCK * k : BLOCK * k + BLOCK].astype(bf16)
-
-        def mine(self):
-            return tuple(bits[axis] for axis in self.route[: self.step])
-
-        def push(self):
-            axis = self.route[self.step]
-            self.copy = send(self.grads.at[(*self.mine(), 1 - bits[axis])], self.landing[self.step], where[axis])
-
-        def pull(self, out=None):
-            self.copy.wait_recv()
-            landing = self.landing[self.step]
-            self.step += 1
-            kept = self.mine()
-            left = 4 - self.step
-
-            def add(i, _):
-                at = tuple((i // 2**k) % 2 for k in range(left))
-                mine, theirs = self.grads[(*kept, *at)], landing[at if at else Ellipsis]
-                if out is None:
-                    self.grads[(*kept, *at)] = mine + theirs
-                else:
-                    out[...] = mine.astype(f32) + theirs.astype(f32)
-                return 0
-
-            if left:
-                lax.fori_loop(0, 2**left, add, 0)
-            else:
-                add(0, 0)
-
-        def turn(self):
-            self.pull()
-            self.push()
-
-    usual = tuple(place)
-    job_down, job_up = Job(R.job0, usual), Job(R.job1, usual)
-    job_out, job_a, job_b = Job(R.job2, usual), Job(R.job3, usual), Job(R.job4, usual)
-
-    def wide(job, left, right):
-        def step(n, _):
-            at = pl.ds(pl.multiple_of(256 * n, 256), 256)
-            job.put(dot(left[...], right[:, at]), at)
-            return 0
-
-        lax.fori_loop(0, 6, step, 0)
-
-    wide(job_down, R.gmlpt, R.act)
-    job_down.push()
 
     kv_in, dq_in = [], []
 
@@ -463,16 +476,22 @@
         dq_in.append(send(R.dqout.at[h], R.dqin.at[h], to_near))
         R.dq[h] = 0.125 * total[0]
 
+    down0.turn()
     back_head(0)
-    job_down.turn()
+    down1.turn()
     back_head(1)
     back_head(2)
     R.norm2t[...] = R.norm2[...].T
-    wide(job_up, R.norm2t, R.gup)
-    job_up.push()
+    for k, job in enumerate((up0, up1)):
+        for n in range(3):
+            at = slice(WIDTH * k + 256 * n, WIDTH * k + 256 * n + 256)
+            job.put(dot(R.norm2t[...], R.gup[:, at]), slice(256 * n, 256 * n + 256))
+        job.push()
+    down0.turn()
     R.mlp[0] = dot(R.act[...], R.wdown[...]).astype(bf16)
     mlp_in = send(R.mlp.at[0], R.mlp.at[1], to_y)
-    job_up.turn()
+    up0.turn()
+    up1.turn()
 
     ghid_in.wait_recv()
 
@@ -489,23 +508,30 @@
     mixed = jnp.concatenate([R.mix[0, (a + m) % 2].reshape(group) for a in range(2)], axis=0)
     job_out.put(dot(R.gattnt[...], mixed, 1, 1), slice(None))
     job_out.push()
+    down1.turn()
     job_out.turn()
-    job_down.turn()
 
     mlp_in.wait_recv()
 
     def block_out(rows):
         both = R.mlp[0, rows].astype(f32) + R.mlp[1, rows].astype(f32) + R.downb[...]
         value = R.hidden[rows] + both
-        R.o_block[rows] = value.astype(bf16)
-        R.o_next[rows] = (R.hacc[rows] + mix_last * value).astype(bf16)
+        R.s_block[rows] = value.astype(bf16)
+        R.s_next[rows] = (R.hacc[rows] + mix_last * value).astype(bf16)
         attn = R.attn[rows]
         for k, term in enumerate((value * R.cotn[rows].astype(f32), value * value, attn * attn, both * both)):
             R.small[0, 6:7, 128 * (2 + k) : 128 * (3 + k)] += 0.5 * folded(term)
 
     row_chunks(ROWS, block_out, 32)
+    for k in range(8):
+        R.small[0, 10 + k // 6 : 11 + k // 6, 128 * (k % 6) : 128 * (k % 6) + 128] = jnp.full((1, 128), R.mixw[k], f32)
+    write(R.s_block, R.o_block)
+    write(R.s_next, R.o_next)
     R.small[0, 8:9] = R.upsum[:, :WIDTH]
     R.small[0, 9:10] = R.upsum[:, WIDTH:]
+
+    up0.turn()
+    down0.turn()
 
     cosine, sine = R.cosine[...], -R.sine[...]
     for h in range(3):
@@ -538,75 +564,109 @@
     job_a.push()
     job_b.put(dot(R.norm1t[...], every[640:], 1, 1), slice(None))
     job_b.push()
+    up1.turn()
+    down1.turn()
     small_in.wait_recv()
     R.small[1, 0:8] = R.small[0, 0:8] + R.smallin[0, 0:8]
     R.small[1, 8:16] = R.small[0, 8:16]
     small_in = send(R.small.at[1], R.smallin.at[1], to_core)
-    job_down.turn()
-    job_up.turn()
+    job_a.turn()
+    job_b.turn()
+    job_out.turn()
+    up0.turn()
     small_in.wait_recv()
     R.small[2] = R.small[1] + R.smallin[1]
     small_in = send(R.small.at[2], R.smallin.at[2], to_x)
+    up1.turn()
+    down0.pull(R.s_down.at[:, pl.ds(0, WIDTH)])
+    down1.pull(R.s_down.at[:, pl.ds(WIDTH, WIDTH)])
+    write(R.s_down, R.o_down)
+    gin_in.wait_recv()
+
+    def grad_in(rows):
+        both = R.gin[0, rows].astype(f32) + R.gin[1, rows].astype(f32)
+        R.s_gin[rows] = (R.gblock[rows] + both).astype(bf16)
+
+    row_chunks(ROWS, grad_in)
+    write(R.s_gin, R.o_gin)
     job_a.turn()
+    job_out.turn()
     job_b.turn()
-    job_out.turn()
     small_in.wait_recv()
     R.small[3] = R.small[2] + R.smallin[2]
     small_in = [
         send(R.small.at[3], R.smallz.at[k], there) for k, there in enumerate((to_near, to_flip, to_far))
     ]
-    job_up.turn()
-    job_out.turn()
-    job_down.pull(R.o_down)
     job_a.turn()
-    job_b.turn()
-    gin_in.wait_recv()
-
-    def grad_in(rows):
-        both = R.gin[0, rows].astype(f32) + R.gin[1, rows].astype(f32)
-        R.o_gin[rows] = (R.gblock[rows] + both).astype(bf16)
-
-    row_chunks(ROWS, grad_in)
-    job_a.turn()
+    up0.pull(R.s_up.at[:, pl.ds(0, WIDTH)])
+    up1.pull(R.s_up.at[:, pl.ds(WIDTH, WIDTH)])
+    write(R.s_up, R.o_up)
+    job_out.pull(R.s_out)
+    write(R.s_out, R.o_out)
     job_b.turn()
     for c in small_in:
         c.wait_recv()
-    R.o_small[...] = (R.small[3] + R.smallz[0]) + (R.smallz[1] + R.smallz[2])
-    job_up.pull(R.o_up)
-    job_out.pull(R.o_out)
-    job_a.pull(R.o_a)
-    job_b.pull(R.o_b)
+    R.s_small[...] = (R.small[3] + R.smallz[0]) + (R.smallz[1] + R.smallz[2])
+    R.s_small[10:12] = R.small[0, 10:12]
+    write(R.s_small, R.o_small)
+    job_a.pull(R.s_a)
+    write(R.s_a, R.o_a)
+    job_b.pull(R.s_b)
+    write(R.s_b, R.o_b)
     for c in started:
         c.wait_send()
+    for c in written:
+        c.wait()
 
 
 def last_kernel(make, entries, *refs):
     R = make(refs)
-    R.next[0] = R.o_next[...]
-    R.block[0] = R.o_block[...]
-    R.gin[0] = R.o_gin[...]
-
-    def history_back(rows):
-        cot = R.cotn[rows].astype(f32)
-        for j in range(8):
-            R.ghist[j, 0, rows] = (R.mixw[j] * cot).astype(bf16)
-
-    row_chunks(ROWS, history_back)
-    R.gq[...] = R.o_a[:, :LOCAL]
-    R.gk[...] = jnp.concatenate([R.o_a[:, LOCAL:], R.o_b[:, :128]], axis=1)
-    R.gv[...] = R.o_b[:, 128:]
-    R.gup[...] = R.o_up[...]
-    R.gout[...] = R.o_out[...]
-    R.gdown[...] = R.o_down[...]
-    for i, ref in enumerate((R.gain1, R.shift1, R.gain2, R.shift2, R.downb)):
-        ref[...] = R.o_small[i]
-    R.upb[0:WIDTH] = R.o_small[8]
-    R.upb[WIDTH:HIDDEN] = R.o_small[9]
-    parts = [R.o_small[5 + k // 6 : 6 + k // 6, 128 * (k % 6) : 128 * (k % 6) + 128] for k in range(12)]
+    copies = []
+
+    def copy(src, dst):
+        moving = pltpu.make_async_copy(src, dst, R.sems.at[len(copies)])
+        moving.start()
+        copies.append(moving)
+        return moving
+
+    get_cot = [copy(R.cotn, R.v_cotn), copy(R.o_small, R.v_small)]
+    pairs = [(R.o_next, R.v_next, R.next.at[0]), (R.o_block, R.v_block, R.block.at[0])]
+    pairs += [(R.o_gin, R.v_gin, R.gin.at[0]), (R.o_up, R.v_up, R.gup), (R.o_down, R.v_down, R.gdown)]
+    pairs.append((R.o_out, R.v_out, R.gout))
+    loads = [copy(src, dst) for src, dst, _ in pairs]
+    loads += [copy(R.o_a, R.v_a), copy(R.o_b, R.v_b)]
+    for c in get_cot:
+        c.wait()
+    count = len(copies)
+    for j in range(8):
+        weight = R.v_small[10 + j // 6 : 11 + j // 6, 128 * (j % 6) : 128 * (j % 6) + 1]
+        R.v_hist[j] = (weight * R.v_cotn[...].astype(f32)).astype(bf16)
+        copy(R.v_hist.at[j], R.ghist.at[j, 0])
+    for c, (_, held, out) in zip(loads, pairs):
+        c.wait()
+        copy(held, out)
+    loads[-2].wait()
+    loads[-1].wait()
+    copy(R.v_a.at[:, pl.ds(0, LOCAL)], R.gq)
+    copy(R.v_a.at[:, pl.ds(LOCAL, 256)], R.gk.at[:, pl.ds(0, 256)])
+    copy(R.v_b.at[:, pl.ds(0, 128)], R.gk.at[:, pl.ds(256, 128)])
+    copy(R.v_b.at[:, pl.ds(128, LOCAL)], R.gv)
+    vectors = (R.gain1, R.shift1, R.gain2, R.shift2, R.downb)
+    for i, ref in enumerate((R.v_gain1, R.v_shift1, R.v_gain2, R.v_shift2, R.v_downb)):
+        ref[...] = R.v_small[i]
+        copy(ref, vectors[i])
+    R.v_upb[0:WIDTH] = R.v_small[8]
+    R.v_upb[WIDTH:HIDDEN] = R.v_small[9]
+    copy(R.v_upb, R.upb)
+    parts = [R.v_small[5 + k // 6 : 6 + k // 6, 128 * (k % 6) : 128 * (k % 6) + 128] for k in range(12)]
     sums = jnp.sum(jnp.concatenate(parts, axis=0), axis=1, keepdims=True)
     row = jnp.broadcast_to(sums, (12, 128)).T[0:1]
-    R.gmix[...] = row[0, :9]
-    R.rms[...] = jnp.sqrt(row / entries)[0, 9:]
+    R.v_gmix[...] = row[0, :9]
+    R.v_rms[...] = jnp.sqrt(row / entries)[0, 9:]
+    copy(R.v_gmix, R.gmix)
+    copy(R.v_rms, R.rms)
+    for c in copies[count:]:
+        c.wait()
 
 
 def out_spec(shape, dtype=f32):
@@ -639,21 +699,21 @@
     cotangent_next,
     cotangent_block,
 ):
-    vmem, hbm, smem = (pl.BlockSpec(memory_space=s) for s in (pltpu.VMEM, pl.ANY, pltpu.SMEM))
+    hbm = pl.BlockSpec(memory_space=pl.ANY)
     args = dict(
-        x=inputs[0], gain1_in=first_gain, shift1_in=first_shift, gain2_in=second_gain, shift2_in=second_shift,
+        x_h=inputs[0], gain1_in=first_gain, shift1_in=first_shift, gain2_in=second_gain, shift2_in=second_shift,
         upb_in=up_bias, downb_in=down_bias,
         cotn_h=cotangent_next[0], cotb_h=cotangent_block[0], wq_h=query_weight, wk_h=key_weight, wv_h=value_weight,
         wout=out_weight.reshape(2, 3, HEAD_DIM, WIDTH), history=history[:, 0], wup_h=up_weight, wdown_h=down_weight,
-        windows=window_lengths[0], order=block_order, mixw=mix_weights,
-    )
-    specs = [vmem] * 7 + [hbm] * 9 + [smem] * 3
+        windows_in=window_lengths[0], order_in=block_order, mixw_in=mix_weights,
+    )
+    specs = [hbm] * len(args)
     outs = dict(
         o_next=out_spec((ROWS, WIDTH), bf16), o_block=out_spec((ROWS, WIDTH), bf16), o_gin=out_spec((ROWS, WIDTH), bf16),
         o_down=out_spec((BLOCK, HIDDEN)), o_up=out_spec((BLOCK, HIDDEN)), o_out=out_spec((BLOCK, LOCAL)),
         o_a=out_spec((BLOCK, 640)), o_b=out_spec((BLOCK, 512)), o_small=out_spec((16, WIDTH)),
     )
-    scratch = scratch_spec()
+    scratch = scratch_spec(window_lengths.shape[1])
     flat, names = [], []
     for name, spec in scratch.items():
         several = isinstance(spec, list)
@@ -671,7 +731,7 @@
         functools.partial(layer_kernel, make),
         out_shape=list(outs.values()),
         in_specs=specs,
-        out_specs=[vmem] * len(outs),
+        out_specs=[hbm] * len(outs),
         scratch_shapes=flat,
         compiler_params=pltpu.CompilerParams(
             collective_id=1, has_side_effects=True, vmem_limit_bytes=63 * 2**20
@@ -688,12 +748,21 @@
         downb=out_spec((WIDTH,)), gmix=out_spec((9,)), rms=out_spec((3,)),
     )
     entries = float(lax.axis_size("batch") * lax.axis_size("seq") * ROWS * WIDTH)
-    given = dict(cotn=cotangent_next[0], mixw=mix_weights, **held)
+    given = dict(cotn=cotangent_next[0], **held)
+    vm, full, row = pltpu.VMEM, pltpu.VMEM((ROWS, WIDTH), bf16), pltpu.VMEM((WIDTH,), f32)
+    staging = dict(
+        v_cotn=full, v_hist=vm((8, ROWS, WIDTH), bf16), v_next=full, v_block=full, v_gin=full,
+        v_up=vm((BLOCK, HIDDEN), f32), v_down=vm((BLOCK, HIDDEN), f32), v_out=vm((BLOCK, LOCAL), f32),
+        v_a=vm((BLOCK, 640), f32), v_b=vm((BLOCK, 512), f32), v_small=vm((16, WIDTH), f32),
+        v_gain1=row, v_shift1=row, v_gain2=row, v_shift2=row, v_downb=row, v_upb=vm((HIDDEN,), f32),
+        v_gmix=vm((9,), f32), v_rms=vm((3,), f32), sems=pltpu.SemaphoreType.DMA((40,)),
+    )
     done = pl.pallas_call(
-        functools.partial(last_kernel, namer(given, results), entries),
+        functools.partial(last_kernel, namer(given, results, staging), entries),
         out_shape=list(results.values()),
-        in_specs=[vmem, smem] + [vmem] * len(held),
-        out_specs=[vmem] * len(results),
+        in_specs=[hbm] * len(given),
+        out_specs=[hbm] * len(results),
+        scratch_shapes=list(staging.values()),
         compiler_params=pltpu.CompilerParams(vmem_limit_bytes=63 * 2**20),
     )(*given.values())
     done = dict(zip(results, done))

time: 104 us -> 97.1 us (0.934)
  Pallas kernels: 103 us -> 96.1 us
    pallas_call x1, Pallas kernels: 98.3 us -> 92.2 us  [per_device_block(): pl.pallas_call(functools.partial(layer_kernel, make), out_shape=list(outs...]
where the time goes in v3:
time: 97.1 us; the launch traced here: 96.9 us
  Pallas kernels  96.1 us (99%)
    pallas_call x1, Pallas kernels, per_device_block(): pl.pallas_call(functools.partial(layer_kernel, make), out_shape=list(outs...  92.2 us
    pallas_call x1, Pallas kernels, per_device_block(): pl.pallas_call(functools.partial(last_kernel, namer(given, results, stagi...  3.85 us

profile of v3, /device:TPU:0, one launch (start us, length us, event | category | flops | bytes accessed | tf_op | source)
XLA Modules:
  0.0 96.9 jit_solution(11105456073093339204)
XLA Ops:
  0.7 92.2 %shard_map.322 = (bf16[256,768]{1,0:T(8,128)(2,1)}, bf16[256,768]{1,0:T(8,128)(2,1)}, bf16[256,768]{1,0:T(8,128)(2,1)}, f32[48,1536]{1,0:T(8,128)}, f32[48,1536]...) custom-call(bf16[256,768]{1,0:T(8,128)(2,1)} %bitcast.12, ...), custom_call_target="tpu_custom_call" | custom-call | tf_op jit(solution)/shard_map/pallas_call | solution.py:730
  92.9 3.8 %shard_map.323 = (bf16[1,256,768]{2,1,0:T(8,128)(2,1)}, bf16[1,256,768]{2,1,0:T(8,128)(2,1)}, bf16[1,256,768]{2,1,0:T(8,128)(2,1)}, bf16[8,1,256,768]{3,2,1,0:T(...) custom-call(bf16[256,768]{1,0:T(8,128)(2,1)} %bitcast.10, ...), custom_call_target="tpu_custom_call" | custom-call | tf_op jit(solution)/shard_map/pallas_call | solution.py:760

commit v4 on v3

--- a/solution.py
+++ b/solution.py
@@ -131,10 +131,10 @@
         dkv=vm((4, 3, 2, HEAD_DIM, ROWS), bf16), dkvin=vm((4, 3, 2, HEAD_DIM, ROWS), bf16),
         dq=vm((3, HEAD_DIM, ROWS), f32), dqout=vm(heads, bf16), dqin=vm(heads, bf16),
         own0=vm((3, 2, HEAD_DIM, ROWS), f32), lin=vm((3, 2, *heads), bf16), gattnt=turned,
-        small=vm((5, 16, WIDTH), f32), smallin=vm((3, 16, WIDTH), f32), smallz=vm((3, 16, WIDTH), f32),
+        small=vm((6, 16, WIDTH), f32), smallin=vm((5, 16, WIDTH), f32), last=vm((6, 16, 128), f32), lastin=vm((5, 16, 128), f32),
         job0=job(WIDTH), job1=job(WIDTH), job2=job(WIDTH), job3=job(WIDTH), job4=job(LOCAL), job5=job(640), job6=job(512),
         s_next=full16, s_block=full16, s_gin=full16, s_down=vm((BLOCK, HIDDEN), f32), s_up=vm((BLOCK, HIDDEN), f32),
-        s_out=vm((BLOCK, LOCAL), f32), s_a=vm((BLOCK, 640), f32), s_b=vm((BLOCK, 512), f32), s_small=vm((16, WIDTH), f32),
+        s_out=vm((BLOCK, LOCAL), f32), s_a=vm((BLOCK, 640), f32), s_b=vm((BLOCK, 512), f32), s_last=vm((16, 128), f32), s_small=vm((16, WIDTH), f32),
         osem=pltpu.SemaphoreType.DMA((12,)),
         ssem=pltpu.SemaphoreType.DMA((96,)), rsem=pltpu.SemaphoreType.DMA((96,)), lsem=pltpu.SemaphoreType.DMA((24,)),
     )
@@ -253,6 +253,7 @@
     for c in get_cot:
         c.wait()
     R.small[0] = jnp.zeros((16, WIDTH), f32)
+    R.last[0] = jnp.zeros((16, 128), f32)
     mix_last = R.mixw[8]
 
     def block_grads(rows):
@@ -260,7 +261,7 @@
         R.gblock[rows] = g
         low = g.astype(bf16)
         R.gmlp[rows] = low
-        R.small[0, 4:5] += 0.5 * jnp.sum(low.astype(f32), axis=0, keepdims=True)
+        R.small[0, 2:3] += 0.5 * jnp.sum(low.astype(f32), axis=0, keepdims=True)
 
     row_chunks(ROWS, block_grads)
     R.gmlpt[...] = R.gmlp[...].T
@@ -273,7 +274,7 @@
         for j in range(8):
             h = R.hist[j, rows].astype(f32)
             total = total + R.mixw[j] * h
-            R.small[0, 5 + j // 6 : 6 + j // 6, 128 * (j % 6) : 128 * (j % 6) + 128] += 0.5 * folded(h * cot)
+            R.small[0, 3 + j // 6 : 4 + j // 6, 128 * (j % 6) : 128 * (j % 6) + 128] += 0.5 * folded(h * cot)
         R.hacc[rows] = total
 
     row_chunks(ROWS, history_sum, 32)
@@ -397,7 +398,8 @@
 
     usual = tuple(place)
     down0, down1, up0, up1 = (Job(bufs, usual) for bufs in (R.job0, R.job1, R.job2, R.job3))
-    job_out, job_a, job_b = (Job(bufs, usual) for bufs in (R.job4, R.job5, R.job6))
+    job_out, job_a = Job(R.job4, usual), Job(R.job5, usual)
+    job_b = Job(R.job6, usual)
 
     row_chunks(ROWS, norm_second)
     for n in range(6):
@@ -445,6 +447,29 @@
             ]
         )
     ghid_in = send(R.ghid.at[0], R.ghid.at[1], to_y)
+
+    class Sum:
+        def __init__(self, held, landing, shared):
+            self.held, self.landing, self.shared, self.step, self.copy = held, landing, shared, 0, None
+
+        def push(self):
+            there = (to_y, to_core, to_near, to_flip, to_x)[self.step]
+            rows = pl.ds(0, self.shared if self.step == 0 else 16)
+            self.copy = send(self.held.at[self.step, rows], self.landing.at[self.step, rows], there)
+
+        def pull(self):
+            self.copy.wait_recv()
+            step, rows = self.step, self.shared if self.step == 0 else 16
+            self.held[step + 1, 0:rows] = self.held[step, 0:rows] + self.landing[step, 0:rows]
+            if rows < 16:
+                self.held[step + 1, rows:16] = self.held[step, rows:16]
+            self.step += 1
+
+        def turn(self):
+            self.pull()
+            self.push()
+
+    sums, last = Sum(R.small, R.smallin, 8), Sum(R.last, R.lastin, 16)
 
     kv_in, dq_in = [], []
 
@@ -476,22 +501,25 @@
         dq_in.append(send(R.dqout.at[h], R.dqin.at[h], to_near))
         R.dq[h] = 0.125 * total[0]
 
-    down0.turn()
-    back_head(0)
-    down1.turn()
-    back_head(1)
-    back_head(2)
-    R.norm2t[...] = R.norm2[...].T
-    for k, job in enumerate((up0, up1)):
+    def up_grads(job, k):
         for n in range(3):
             at = slice(WIDTH * k + 256 * n, WIDTH * k + 256 * n + 256)
             job.put(dot(R.norm2t[...], R.gup[:, at]), slice(256 * n, 256 * n + 256))
         job.push()
+
+    down0.turn()
+    R.norm2t[...] = R.norm2[...].T
+    up_grads(up0, 0)
+    down1.turn()
+    back_head(0)
+    up_grads(up1, 1)
+    back_head(1)
+    up0.turn()
+    back_head(2)
+    up1.turn()
     down0.turn()
     R.mlp[0] = dot(R.act[...], R.wdown[...]).astype(bf16)
     mlp_in = send(R.mlp.at[0], R.mlp.at[1], to_y)
-    up0.turn()
-    up1.turn()
 
     ghid_in.wait_recv()
 
@@ -500,8 +528,8 @@
         R.gblock[rows] = hid
         R.gmlp[rows] = hid.astype(bf16)
         back = R.gnorm2[rows]
-        R.small[0, 2:3] += jnp.sum(back * R.unit2[rows], axis=0, keepdims=True)
-        R.small[0, 3:4] += jnp.sum(back, axis=0, keepdims=True)
+        R.small[0, 0:1] += jnp.sum(back * R.unit2[rows], axis=0, keepdims=True)
+        R.small[0, 1:2] += jnp.sum(back, axis=0, keepdims=True)
 
     row_chunks(ROWS, whole_hidden)
     R.gattnt[...] = R.gmlp[...].T
@@ -511,6 +539,9 @@
     down1.turn()
     job_out.turn()
 
+    up0.turn()
+    down0.turn()
+
     mlp_in.wait_recv()
 
     def block_out(rows):
@@ -520,7 +551,7 @@
         R.s_next[rows] = (R.hacc[rows] + mix_last * value).astype(bf16)
         attn = R.attn[rows]
         for k, term in enumerate((value * R.cotn[rows].astype(f32), value * value, attn * attn, both * both)):
-            R.small[0, 6:7, 128 * (2 + k) : 128 * (3 + k)] += 0.5 * folded(term)
+            R.small[0, 4:5, 128 * (2 + k) : 128 * (3 + k)] += 0.5 * folded(term)
 
     row_chunks(ROWS, block_out, 32)
     for k in range(8):
@@ -530,8 +561,7 @@
     R.small[0, 8:9] = R.upsum[:, :WIDTH]
     R.small[0, 9:10] = R.upsum[:, WIDTH:]
 
-    up0.turn()
-    down0.turn()
+    sums.push()
 
     cosine, sine = R.cosine[...], -R.sine[...]
     for h in range(3):
@@ -553,34 +583,35 @@
     def first_back(rows):
         grad = R.gnew[rows]
         R.gin[0, rows] = norm_back(grad, R.unit1[rows], R.inv1[rows], R.gain1[...]).astype(bf16)
-        R.small[0, 0:1] += jnp.sum(grad * R.unit1[rows], axis=0, keepdims=True)
-        R.small[0, 1:2] += jnp.sum(grad, axis=0, keepdims=True)
+        for i, term in enumerate((grad * R.unit1[rows], grad)):
+            total = jnp.sum(term, axis=0, keepdims=True)
+            for k in range(6):
+                R.last[0, 6 * i + k : 6 * i + k + 1] += total[:, 128 * k : 128 * k + 128]
 
     row_chunks(ROWS, first_back)
-    small_in = send(R.small.at[0, pl.ds(0, 8)], R.smallin.at[0, pl.ds(0, 8)], to_y)
+    last.push()
     gin_in = send(R.gin.at[0], R.gin.at[1], to_y)
     every = jnp.concatenate(lins, axis=0)
     job_a.put(dot(R.norm1t[...], every[:640], 1, 1), slice(None))
     job_a.push()
     job_b.put(dot(R.norm1t[...], every[640:], 1, 1), slice(None))
     job_b.push()
+    sums.turn()
     up1.turn()
     down1.turn()
-    small_in.wait_recv()
-    R.small[1, 0:8] = R.small[0, 0:8] + R.smallin[0, 0:8]
-    R.small[1, 8:16] = R.small[0, 8:16]
-    small_in = send(R.small.at[1], R.smallin.at[1], to_core)
+    last.turn()
+    sums.turn()
     job_a.turn()
     job_b.turn()
+    last.turn()
     job_out.turn()
     up0.turn()
-    small_in.wait_recv()
-    R.small[2] = R.small[1] + R.smallin[1]
-    small_in = send(R.small.at[2], R.smallin.at[2], to_x)
-    up1.turn()
     down0.pull(R.s_down.at[:, pl.ds(0, WIDTH)])
     down1.pull(R.s_down.at[:, pl.ds(WIDTH, WIDTH)])
     write(R.s_down, R.o_down)
+    sums.turn()
+    last.turn()
+    up1.turn()
     gin_in.wait_recv()
 
     def grad_in(rows):
@@ -591,24 +622,23 @@
     write(R.s_gin, R.o_gin)
     job_a.turn()
     job_out.turn()
+    sums.turn()
+    last.turn()
     job_b.turn()
-    small_in.wait_recv()
-    R.small[3] = R.small[2] + R.smallin[2]
-    small_in = [
-        send(R.small.at[3], R.smallz.at[k], there) for k, there in enumerate((to_near, to_flip, to_far))
-    ]
-    job_a.turn()
     up0.pull(R.s_up.at[:, pl.ds(0, WIDTH)])
     up1.pull(R.s_up.at[:, pl.ds(WIDTH, WIDTH)])
     write(R.s_up, R.o_up)
+    job_a.turn()
+    job_b.turn()
     job_out.pull(R.s_out)
     write(R.s_out, R.o_out)
-    job_b.turn()
-    for c in small_in:
-        c.wait_recv()
-    R.s_small[...] = (R.small[3] + R.smallz[0]) + (R.smallz[1] + R.smallz[2])
+    sums.pull()
+    R.s_small[...] = R.small[5]
     R.s_small[10:12] = R.small[0, 10:12]
     write(R.s_small, R.o_small)
+    last.pull()
+    R.s_last[...] = R.last[5]
+    write(R.s_last, R.o_last)
     job_a.pull(R.s_a)
     write(R.s_a, R.o_a)
     job_b.pull(R.s_b)
@@ -629,7 +659,7 @@
         copies.append(moving)
         return moving
 
-    get_cot = [copy(R.cotn, R.v_cotn), copy(R.o_small, R.v_small)]
+    get_cot = [copy(R.cotn, R.v_cotn), copy(R.o_small, R.v_small), copy(R.o_last, R.v_last)]
     pairs = [(R.o_next, R.v_next, R.next.at[0]), (R.o_block, R.v_block, R.block.at[0])]
     pairs += [(R.o_gin, R.v_gin, R.gin.at[0]), (R.o_up, R.v_up, R.gup), (R.o_down, R.v_down, R.gdown)]
     pairs.append((R.o_out, R.v_out, R.gout))
@@ -651,14 +681,20 @@
     copy(R.v_a.at[:, pl.ds(LOCAL, 256)], R.gk.at[:, pl.ds(0, 256)])
     copy(R.v_b.at[:, pl.ds(0, 128)], R.gk.at[:, pl.ds(256, 128)])
     copy(R.v_b.at[:, pl.ds(128, LOCAL)], R.gv)
-    vectors = (R.gain1, R.shift1, R.gain2, R.shift2, R.downb)
-    for i, ref in enumerate((R.v_gain1, R.v_shift1, R.v_gain2, R.v_shift2, R.v_downb)):
+    for k in range(6):
+        R.v_gain1[128 * k : 128 * k + 128] = R.v_last[k]
+        R.v_shift1[128 * k : 128 * k + 128] = R.v_last[6 + k]
+    for i, ref in enumerate((R.v_gain2, R.v_shift2, R.v_downb)):
         ref[...] = R.v_small[i]
-        copy(ref, vectors[i])
+    copy(R.v_gain1, R.gain1)
+    copy(R.v_shift1, R.shift1)
+    copy(R.v_gain2, R.gain2)
+    copy(R.v_shift2, R.shift2)
+    copy(R.v_downb, R.downb)
     R.v_upb[0:WIDTH] = R.v_small[8]
     R.v_upb[WIDTH:HIDDEN] = R.v_small[9]
     copy(R.v_upb, R.upb)
-    parts = [R.v_small[5 + k // 6 : 6 + k // 6, 128 * (k % 6) : 128 * (k % 6) + 128] for k in range(12)]
+    parts = [R.v_small[3 + k // 6 : 4 + k // 6, 128 * (k % 6) : 128 * (k % 6) + 128] for k in range(12)]
     sums = jnp.sum(jnp.concatenate(parts, axis=0), axis=1, keepdims=True)
     row = jnp.broadcast_to(sums, (12, 128)).T[0:1]
     R.v_gmix[...] = row[0, :9]
@@ -711,7 +747,7 @@
     outs = dict(
         o_next=out_spec((ROWS, WIDTH), bf16), o_block=out_spec((ROWS, WIDTH), bf16), o_gin=out_spec((ROWS, WIDTH), bf16),
         o_down=out_spec((BLOCK, HIDDEN)), o_up=out_spec((BLOCK, HIDDEN)), o_out=out_spec((BLOCK, LOCAL)),
-        o_a=out_spec((BLOCK, 640)), o_b=out_spec((BLOCK, 512)), o_small=out_spec((16, WIDTH)),
+        o_a=out_spec((BLOCK, 640)), o_b=out_spec((BLOCK, 512)), o_small=out_spec((16, WIDTH)), o_last=out_spec((16, 128)),
     )
     scratch = scratch_spec(window_lengths.shape[1])
     flat, names = [], []
@@ -753,7 +789,7 @@
     staging = dict(
         v_cotn=full, v_hist=vm((8, ROWS, WIDTH), bf16), v_next=full, v_block=full, v_gin=full,
         v_up=vm((BLOCK, HIDDEN), f32), v_down=vm((BLOCK, HIDDEN), f32), v_out=vm((BLOCK, LOCAL), f32),
-        v_a=vm((BLOCK, 640), f32), v_b=vm((BLOCK, 512), f32), v_small=vm((16, WIDTH), f32),
+        v_a=vm((BLOCK, 640), f32), v_b=vm((BLOCK, 512), f32), v_small=vm((16, WIDTH), f32), v_last=vm((16, 128), f32),
         v_gain1=row, v_shift1=row, v_gain2=row, v_shift2=row, v_downb=row, v_upb=vm((HIDDEN,), f32),
         v_gmix=vm((9,), f32), v_rms=vm((3,), f32), sems=pltpu.SemaphoreType.DMA((40,)),
     )

time: 97.1 us -> 96.6 us (level)
  no operation moved by 1% of the time
where the time goes in v4:
time: 96.6 us; the launch traced here: 96.4 us
  Pallas kernels  95.6 us (99%)
    pallas_call x1, Pallas kernels, per_device_block(): pl.pallas_call(functools.partial(layer_kernel, make), out_shape=list(outs...  91.7 us
    pallas_call x1, Pallas kernels, per_device_block(): pl.pallas_call(functools.partial(last_kernel, namer(given, results, stagi...  3.85 us

profile of v4, /device:TPU:0, one launch (start us, length us, event | category | flops | bytes accessed | tf_op | source)
XLA Modules:
  0.0 96.4 jit_solution(7449063191016534098)
XLA Ops:
  0.7 91.7 %shard_map.322 = (bf16[256,768]{1,0:T(8,128)(2,1)}, bf16[256,768]{1,0:T(8,128)(2,1)}, bf16[256,768]{1,0:T(8,128)(2,1)}, f32[48,1536]{1,0:T(8,128)}, f32[48,1536]...) custom-call(bf16[256,768]{1,0:T(8,128)(2,1)} %bitcast.12, ...), custom_call_target="tpu_custom_call" | custom-call | tf_op jit(solution)/shard_map/pallas_call | solution.py:766
  92.4 3.8 %shard_map.323 = (bf16[1,256,768]{2,1,0:T(8,128)(2,1)}, bf16[1,256,768]{2,1,0:T(8,128)(2,1)}, bf16[1,256,768]{2,1,0:T(8,128)(2,1)}, bf16[8,1,256,768]{3,2,1,0:T(...) custom-call(bf16[256,768]{1,0:T(8,128)(2,1)} %bitcast.10, ...), custom_call_target="tpu_custom_call" | custom-call | tf_op jit(solution)/shard_map/pallas_call | solution.py:796

commit v5 on v4

--- a/solution.py
+++ b/solution.py
@@ -132,9 +132,9 @@
         dq=vm((3, HEAD_DIM, ROWS), f32), dqout=vm(heads, bf16), dqin=vm(heads, bf16),
         own0=vm((3, 2, HEAD_DIM, ROWS), f32), lin=vm((3, 2, *heads), bf16), gattnt=turned,
         small=vm((6, 16, WIDTH), f32), smallin=vm((5, 16, WIDTH), f32), last=vm((6, 16, 128), f32), lastin=vm((5, 16, 128), f32),
-        job0=job(WIDTH), job1=job(WIDTH), job2=job(WIDTH), job3=job(WIDTH), job4=job(LOCAL), job5=job(640), job6=job(512),
+        job0=job(WIDTH), job1=job(WIDTH), job2=job(WIDTH), job3=job(WIDTH), job4=job(LOCAL), job5=job(WIDTH), job6=job(LOCAL),
         s_next=full16, s_block=full16, s_gin=full16, s_down=vm((BLOCK, HIDDEN), f32), s_up=vm((BLOCK, HIDDEN), f32),
-        s_out=vm((BLOCK, LOCAL), f32), s_a=vm((BLOCK, 640), f32), s_b=vm((BLOCK, 512), f32), s_last=vm((16, 128), f32), s_small=vm((16, WIDTH), f32),
+        s_out=vm((BLOCK, LOCAL), f32), s_a=vm((BLOCK, WIDTH), f32), s_b=vm((BLOCK, LOCAL), f32), s_last=vm((16, 128), f32), s_small=vm((16, WIDTH), f32),
         osem=pltpu.SemaphoreType.DMA((12,)),
         ssem=pltpu.SemaphoreType.DMA((96,)), rsem=pltpu.SemaphoreType.DMA((96,)), lsem=pltpu.SemaphoreType.DMA((24,)),
     )
@@ -592,9 +592,9 @@
     last.push()
     gin_in = send(R.gin.at[0], R.gin.at[1], to_y)
     every = jnp.concatenate(lins, axis=0)
-    job_a.put(dot(R.norm1t[...], every[:640], 1, 1), slice(None))
+    job_a.put(dot(R.norm1t[...], every[:WIDTH], 1, 1), slice(None))
     job_a.push()
-    job_b.put(dot(R.norm1t[...], every[640:], 1, 1), slice(None))
+    job_b.put(dot(R.norm1t[...], every[WIDTH:], 1, 1), slice(None))
     job_b.push()
     sums.turn()
     up1.turn()
@@ -678,9 +678,8 @@
     loads[-2].wait()
     loads[-1].wait()
     copy(R.v_a.at[:, pl.ds(0, LOCAL)], R.gq)
-    copy(R.v_a.at[:, pl.ds(LOCAL, 256)], R.gk.at[:, pl.ds(0, 256)])
-    copy(R.v_b.at[:, pl.ds(0, 128)], R.gk.at[:, pl.ds(256, 128)])
-    copy(R.v_b.at[:, pl.ds(128, LOCAL)], R.gv)
+    copy(R.v_a.at[:, pl.ds(LOCAL, LOCAL)], R.gk)
+    copy(R.v_b, R.gv)
     for k in range(6):
         R.v_gain1[128 * k : 128 * k + 128] = R.v_last[k]
         R.v_shift1[128 * k : 128 * k + 128] = R.v_last[6 + k]
@@ -747,7 +746,7 @@
     outs = dict(
         o_next=out_spec((ROWS, WIDTH), bf16), o_block=out_spec((ROWS, WIDTH), bf16), o_gin=out_spec((ROWS, WIDTH), bf16),
         o_down=out_spec((BLOCK, HIDDEN)), o_up=out_spec((BLOCK, HIDDEN)), o_out=out_spec((BLOCK, LOCAL)),
-        o_a=out_spec((BLOCK, 640)), o_b=out_spec((BLOCK, 512)), o_small=out_spec((16, WIDTH)), o_last=out_spec((16, 128)),
+        o_a=out_spec((BLOCK, WIDTH)), o_b=out_spec((BLOCK, LOCAL)), o_small=out_spec((16, WIDTH)), o_last=out_spec((16, 128)),
     )
     scratch = scratch_spec(window_lengths.shape[1])
     flat, names = [], []
@@ -789,7 +788,7 @@
     staging = dict(
         v_cotn=full, v_hist=vm((8, ROWS, WIDTH), bf16), v_next=full, v_block=full, v_gin=full,
         v_up=vm((BLOCK, HIDDEN), f32), v_down=vm((BLOCK, HIDDEN), f32), v_out=vm((BLOCK, LOCAL), f32),
-        v_a=vm((BLOCK, 640), f32), v_b=vm((BLOCK, 512), f32), v_small=vm((16, WIDTH), f32), v_last=vm((16, 128), f32),
+        v_a=vm((BLOCK, WIDTH), f32), v_b=vm((BLOCK, LOCAL), f32), v_small=vm((16, WIDTH), f32), v_last=vm((16, 128), f32),
         v_gain1=row, v_shift1=row, v_gain2=row, v_shift2=row, v_downb=row, v_upb=vm((HIDDEN,), f32),
         v_gmix=vm((9,), f32), v_rms=vm((3,), f32), sems=pltpu.SemaphoreType.DMA((40,)),
     )

time: 96.6 us -> 96.7 us (level)
  no operation moved by 1% of the time
where the time goes in v5:
time: 96.7 us; the launch traced here: 96.5 us
  Pallas kernels  95.7 us (99%)
    pallas_call x1, Pallas kernels, per_device_block(): pl.pallas_call(functools.partial(layer_kernel, make), out_shape=list(outs...  91.8 us
    pallas_call x1, Pallas kernels, per_device_block(): pl.pallas_call(functools.partial(last_kernel, namer(given, results, stagi...  3.85 us

profile of v5, /device:TPU:0, one launch (start us, length us, event | category | flops | bytes accessed | tf_op | source)
XLA Modules:
  0.0 96.5 jit_solution(14225521022933965442)
XLA Ops:
  0.7 91.8 %shard_map.322 = (bf16[256,768]{1,0:T(8,128)(2,1)}, bf16[256,768]{1,0:T(8,128)(2,1)}, bf16[256,768]{1,0:T(8,128)(2,1)}, f32[48,1536]{1,0:T(8,128)}, f32[48,1536]...) custom-call(bf16[256,768]{1,0:T(8,128)(2,1)} %bitcast.12, ...), custom_call_target="tpu_custom_call" | custom-call | tf_op jit(solution)/shard_map/pallas_call | solution.py:765
  92.5 3.8 %shard_map.323 = (bf16[1,256,768]{2,1,0:T(8,128)(2,1)}, bf16[1,256,768]{2,1,0:T(8,128)(2,1)}, bf16[1,256,768]{2,1,0:T(8,128)(2,1)}, bf16[8,1,256,768]{3,2,1,0:T(...) custom-call(bf16[256,768]{1,0:T(8,128)(2,1)} %bitcast.10, ...), custom_call_target="tpu_custom_call" | custom-call | tf_op jit(solution)/shard_map/pallas_call | solution.py:795
